TPU v7x, 32 devices: a whole 2x2x4 slice. The times are simulated.
32 devices in a mesh: row: 4 (over y, x), col: 8 (over z, core).
Axes of the slice: x: 2, y: 2, z: 4, core: 2. Of those that a mesh axis runs over, the one named last changes fastest.
Arguments:
- tokens: bfloat16 [256, 8192], P('col', 'row'), may hold values from -500 to 500
- norm_gain: float32 [8192], P('row'), may hold values from 0.5 to 1.5
- cotangent: bfloat16 [256, 8192], P('col', 'row'), may hold values from -6 to 6
- gate_frozen_weight: bfloat16 [8192, 28672], P('row', 'col'), may hold values from -0.0625 to 0.0625
- up_frozen_weight: bfloat16 [8192, 28672], P('row', 'col'), may hold values from -0.0625 to 0.0625
- down_frozen_weight: bfloat16 [28672, 8192], P('col', 'row'), may hold values from -0.03125 to 0.03125
- gate_input_factor: bfloat16 [8192, 64], P('row'), may hold values from -0.0625 to 0.0625
- gate_output_factor: bfloat16 [64, 28672], P(None, 'col'), may hold values from -0.75 to 0.75
- up_input_factor: bfloat16 [8192, 64], P('row'), may hold values from -0.0625 to 0.0625
- up_output_factor: bfloat16 [64, 28672], P(None, 'col'), may hold values from -0.75 to 0.75
- down_input_factor: bfloat16 [28672, 64], P('col'), may hold values from -0.03125 to 0.03125
- down_b: bfloat16 [64, 8192], P(None, 'row'), may hold values from -0.75 to 0.75
- gate_input_factor_direction: bfloat16 [8192, 64], P('row'), may hold values from -0.0625 to 0.0625
- gate_output_factor_direction: bfloat16 [64, 28672], P(None, 'col'), may hold values from -0.75 to 0.75
- up_input_factor_direction: bfloat16 [8192, 64], P('row'), may hold values from -0.0625 to 0.0625
- up_output_factor_direction: bfloat16 [64, 28672], P(None, 'col'), may hold values from -0.75 to 0.75
- down_input_factor_direction: bfloat16 [28672, 64], P('col'), may hold values from -0.03125 to 0.03125
- down_b_dir: bfloat16 [64, 8192], P(None, 'row'), may hold values from -0.75 to 0.75
Outputs:
- normed_feature_adjoint: float32 [256, 8192], P('col', 'row')
- normed_feature_adjoint_direction: float32 [256, 8192], P('col', 'row')
- curvature_gate_input: float32 [8192, 64], P('row')
- curvature_gate_output: float32 [64, 28672], P(None, 'col')
- curvature_up_input: float32 [8192, 64], P('row')
- curvature_up_output: float32 [64, 28672], P(None, 'col')
- curvature_down_input: float32 [28672, 64], P('col')
- curvature_down_output: float32 [64, 8192], P(None, 'row')
All inputs are finite; a program needn't handle non-finite values.
Results may differ from a plain program's by a relative error of at most 0.024.
Values may be sent and summed in bfloat16 or wider, within the bound.
A program may use at most 128 MiB of HBM per device.

v0:
```python
import jax
import jax.numpy as jnp
from jax import lax
from jax.sharding import PartitionSpec as P

D = 8192


adapter_scale = 0.5
epsilon = 1e-05


def curvature_product(left, right):
    return jnp.dot(left, right, preferred_element_type=jnp.float32)


def cross_shard_total(left, right):
    return lax.dot_general(
        left, right, (((1,), (1,)), ((), ())), preferred_element_type=jnp.float32
    )


def summed_over_rows(left, right):
    return lax.dot_general(
        left, right, (((0,), (0,)), ((), ())), preferred_element_type=jnp.float32
    )


def lowered(factor, panel):
    return lax.dot_general(
        factor, panel, (((0,), (1,)), ((), ())), preferred_element_type=jnp.float32
    )


def lifted(adjoint, factor):
    return lax.dot_general(
        adjoint, factor, (((0,), (1,)), ((), ())), precision=lax.Precision.HIGHEST
    )


def second_order(
    gate_preactivation,
    up_preactivation,
    hidden_adjoint,
    gate_tangent_rows,
    up_tangent_rows,
    adjoint_tangent_rows,
):
    sigma = jax.nn.sigmoid(gate_preactivation)
    silu_value = gate_preactivation * sigma
    slope = sigma * (1.0 + gate_preactivation * (1.0 - sigma))
    bend = sigma * (1.0 - sigma) * (2.0 + gate_preactivation * (1.0 - 2.0 * sigma))
    hidden_activation = (silu_value * up_preactivation).astype(jnp.bfloat16)
    hidden_direction = (
        slope * gate_tangent_rows * up_preactivation + silu_value * up_tangent_rows
    ).astype(jnp.bfloat16)
    gate_derivative = (hidden_adjoint * up_preactivation * slope).astype(jnp.bfloat16)
    up_derivative = (hidden_adjoint * silu_value).astype(jnp.bfloat16)
    gate_derivative_direction = (
        adjoint_tangent_rows * up_preactivation * slope
        + hidden_adjoint * (up_tangent_rows * slope + up_preactivation * bend * gate_tangent_rows)
    ).astype(jnp.bfloat16)
    up_derivative_direction = (
        adjoint_tangent_rows * silu_value + hidden_adjoint * slope * gate_tangent_rows
    ).astype(jnp.bfloat16)
    return (
        hidden_activation,
        hidden_direction,
        gate_derivative,
        up_derivative,
        gate_derivative_direction,
        up_derivative_direction,
    )


def on_device(
    tokens,
    norm_gain,
    cotangent,
    gate_frozen_weight,
    up_frozen_weight,
    down_frozen_weight,
    gate_input_factor,
    gate_output_factor,
    up_input_factor,
    up_output_factor,
    down_input_factor,
    down_b,
    gate_input_factor_direction,
    gate_output_factor_direction,
    up_input_factor_direction,
    up_output_factor_direction,
    down_input_factor_direction,
    down_b_dir,
):
    rank_size = gate_input_factor.shape[1]
    width_rows = gate_frozen_weight.shape[0]
    width_columns = gate_frozen_weight.shape[1]
    own_count = tokens.shape[0]
    tokens_f = tokens.astype(jnp.float32)
    squares = lax.psum(jnp.sum(tokens_f * tokens_f, axis=1), "row")
    own_normed = (tokens_f * lax.rsqrt(squares[:, None] / D + epsilon) * norm_gain).astype(
        jnp.bfloat16
    )
    normed_tokens, cot_panel = (
        lax.all_gather(own_normed, "col", axis=0, tiled=True),
        lax.all_gather(cotangent, "col", axis=0, tiled=True),
    )
    in_factors = jnp.concatenate(
        [
            gate_input_factor,
            up_input_factor,
            gate_input_factor_direction,
            up_input_factor_direction,
        ],
        axis=1,
    )
    out_factors = jnp.concatenate([down_b, down_b_dir], axis=0)
    projected = jnp.concatenate(
        [curvature_product(normed_tokens, in_factors), cross_shard_total(cot_panel, out_factors)],
        axis=1,
    )
    ranks = lax.psum(projected, "row").astype(jnp.bfloat16)
    swiglu_block = lax.psum(
        jnp.concatenate(
            [
                curvature_product(normed_tokens, gate_frozen_weight),
                curvature_product(normed_tokens, up_frozen_weight),
                cross_shard_total(cot_panel, down_frozen_weight),
            ],
            axis=1,
        ),
        "row",
    )

    def column(array, index):
        return array[:, index * rank_size : (index + 1) * rank_size]

    (
        gate_rank_rows,
        up_rank_rows,
        gate_rank_rows_direction,
        up_rank_rows_direction,
        adjoint_rank_rows,
        adjoint_rank_rows_direction,
    ) = [column(ranks, index) for index in range(6)]
    gate_preactivation = swiglu_block[:, :width_columns] + adapter_scale * curvature_product(
        gate_rank_rows, gate_output_factor
    )
    up_preactivation = swiglu_block[
        :, width_columns : 2 * width_columns
    ] + adapter_scale * curvature_product(up_rank_rows, up_output_factor)
    hidden_adjoint = swiglu_block[:, 2 * width_columns :] + adapter_scale * cross_shard_total(
        adjoint_rank_rows, down_input_factor
    )
    gate_tangent_rows = adapter_scale * (
        curvature_product(gate_rank_rows_direction, gate_output_factor)
        + curvature_product(gate_rank_rows, gate_output_factor_direction)
    )
    up_tangent_rows = adapter_scale * (
        curvature_product(up_rank_rows_direction, up_output_factor)
        + curvature_product(up_rank_rows, up_output_factor_direction)
    )
    adjoint_tangent_rows = adapter_scale * (
        cross_shard_total(adjoint_rank_rows_direction, down_input_factor)
        + cross_shard_total(adjoint_rank_rows, down_input_factor_direction)
    )
    (
        hidden_activation,
        hidden_direction,
        gate_derivative,
        up_derivative,
        gate_derivative_direction,
        up_derivative_direction,
    ) = second_order(
        gate_preactivation,
        up_preactivation,
        hidden_adjoint,
        gate_tangent_rows,
        up_tangent_rows,
        adjoint_tangent_rows,
    )
    (
        gate_full_rows,
        up_full_rows,
        gate_full_rows_direction,
        up_full_rows_direction,
        adjoint_full_rows,
        adjoint_full_rows_direction,
    ) = [column(ranks, index) for index in range(6)]
    curvature_gate_output = adapter_scale * (
        summed_over_rows(gate_full_rows_direction, gate_derivative)
        + summed_over_rows(gate_full_rows, gate_derivative_direction)
    )
    curvature_up_output = adapter_scale * (
        summed_over_rows(up_full_rows_direction, up_derivative)
        + summed_over_rows(up_full_rows, up_derivative_direction)
    )
    curvature_down_input = adapter_scale * (
        summed_over_rows(hidden_direction, adjoint_full_rows)
        + summed_over_rows(hidden_activation, adjoint_full_rows_direction)
    )
    rank_adjoints = jnp.concatenate(
        [
            cross_shard_total(gate_output_factor, gate_derivative),
            cross_shard_total(up_output_factor, up_derivative),
            cross_shard_total(gate_output_factor, gate_derivative_direction)
            + cross_shard_total(gate_output_factor_direction, gate_derivative),
            cross_shard_total(up_output_factor, up_derivative_direction)
            + cross_shard_total(up_output_factor_direction, up_derivative),
            lowered(down_input_factor, hidden_direction)
            + lowered(down_input_factor_direction, hidden_activation),
        ],
        axis=0,
    )
    factors_f = [
        factor.astype(jnp.float32)
        for factor in (
            gate_input_factor,
            up_input_factor,
            gate_input_factor_direction,
            up_input_factor_direction,
        )
    ]
    normed_f = normed_tokens.astype(jnp.float32)
    cotangent_float = cot_panel.astype(jnp.float32)
    adjoints = lax.psum(rank_adjoints.astype(jnp.bfloat16), "col").astype(jnp.float32)
    adjoint_contribution = cross_shard_total(
        gate_derivative, gate_frozen_weight
    ) + cross_shard_total(up_derivative, up_frozen_weight)
    tangent_contribution = cross_shard_total(
        gate_derivative_direction, gate_frozen_weight
    ) + cross_shard_total(up_derivative_direction, up_frozen_weight)
    adjoint_contribution, tangent_contribution = (adjoint_contribution, tangent_contribution)
    summed = lax.psum_scatter(
        jnp.concatenate([adjoint_contribution, tangent_contribution], axis=1).astype(jnp.bfloat16),
        "col",
        scatter_dimension=0,
        tiled=True,
    ).astype(jnp.float32)
    normed_feature_adjoint = summed[:, :width_rows]
    normed_feature_adjoint_direction = summed[:, width_rows:]
    piece = lax.dynamic_slice_in_dim(adjoints, lax.axis_index("col") * own_count, own_count, 1)
    parts = [piece[index * rank_size : (index + 1) * rank_size] for index in range(5)]
    adjoint_contribution = lifted(parts[0], factors_f[0]) + lifted(parts[1], factors_f[1])
    tangent_contribution = (
        lifted(parts[2], factors_f[0])
        + lifted(parts[0], factors_f[2])
        + lifted(parts[3], factors_f[1])
        + lifted(parts[1], factors_f[3])
    )
    normed_feature_adjoint = normed_feature_adjoint + adapter_scale * adjoint_contribution
    normed_feature_adjoint_direction = (
        normed_feature_adjoint_direction + adapter_scale * tangent_contribution
    )
    spread = (((0,), (1,)), ((), ()))
    gate_dir_rows = adjoints[2 * rank_size : 3 * rank_size]
    up_dir_rows = adjoints[3 * rank_size : 4 * rank_size]
    rank_row_values = adjoints[4 * rank_size : 5 * rank_size]
    gate_contribution = adapter_scale * lax.dot_general(
        normed_f, gate_dir_rows, spread, precision=lax.Precision.HIGHEST
    )
    up_contribution = adapter_scale * lax.dot_general(
        normed_f, up_dir_rows, spread, precision=lax.Precision.HIGHEST
    )
    down_contribution = adapter_scale * jnp.dot(
        rank_row_values, cotangent_float, precision=lax.Precision.HIGHEST
    )
    return (
        normed_feature_adjoint,
        normed_feature_adjoint_direction,
        gate_contribution,
        curvature_gate_output,
        up_contribution,
        curvature_up_output,
        curvature_down_input,
        down_contribution,
    )


def solution(mesh):
    in_specs = (
        P("col", "row"),
        P("row"),
        P("col", "row"),
        P("row", "col"),
        P("row", "col"),
        P("col", "row"),
        P("row", None),
        P(None, "col"),
        P("row", None),
        P(None, "col"),
        P("col", None),
        P(None, "row"),
        P("row", None),
        P(None, "col"),
        P("row", None),
        P(None, "col"),
        P("col", None),
        P(None, "row"),
    )
    out_specs = (
        P("col", "row"),
        P("col", "row"),
        P("row", None),
        P(None, "col"),
        P("row", None),
        P(None, "col"),
        P("col", None),
        P(None, "row"),
    )
    return jax.shard_map(
        on_device, mesh=mesh, in_specs=in_specs, out_specs=out_specs, check_vma=False
    )
```

profile of v0, /device:TPU:0, one launch (start us, length us, event | category | flops | bytes accessed | tf_op | source)
XLA Modules:
  0.0 468.7 jit_solution(18091516543193688266)
XLA Ops:
  7.2 0.0 all-gather.3.cloned.1.call-start
  7.2 1.1 fusion.49
  8.3 11.4 %psum.28 = f32[32]{0:T(128)S(1)} all-reduce(f32[32]{0:T(128)S(1)} %fusion.49), channel_id=1, replica_groups=mesh['row'=4,'col'=8] {'row'}, use_global_device_ids=true, to_apply=%region_1.0 | all-reduce | flops 32 | bytes 256 | tf_op jit(solution)/shard_map/psum | solution.py:101
  19.7 1.7 fusion.51
  21.4 0.0 all-gather.3.cloned.1.call-update
  21.4 0.0 all-gather.5.cloned.1.call-start
  21.4 0.7 all-gather.5.cloned.1.call-update
  22.1 0.0 all-reduce.4.cloned.1.call-start
  22.2 21.0 %all-gather.3.cloned.1.call-done = bf16[256,2048]{1,0:T(8,128)(2,1)} async-done(((bf16[32,2048]{1,0:T(8,128)(2,1)}), bf16[256,2048]{1,0:T(8,128)(2,1)}) %all-gather.3.cloned.1.call-update) | async-done | bytes 1048592 | tf_op jit(solution)/shard_map/all_gather | solution.py:106
  43.2 11.5 %fusion.88 = f32[256,3584]{1,0:T(8,128)} fusion(bf16[256,2048]{1,0:T(8,128)(2,1)} %all-gather.3.cloned.1.call-done, bf16[2048,3584]{1,0:T(8,128)(2,1)} %param.21), kind=kOutput, calls=%fused_computation.126 | convolution fusion | flops 3758096384 | bytes 19398656 | tf_op jit(solution)/shard_map/dot_general | solution.py:14
  54.6 9.2 %fusion.89 = f32[256,3584]{1,0:T(8,128)} fusion(bf16[256,2048]{1,0:T(8,128)(2,1)S(1)} %copy-done.10, bf16[2048,3584]{1,0:T(8,128)(2,1)} %param.22), kind=kOutput, calls=%fused_computation.127 | convolution fusion | flops 3758096384 | bytes 19398656 | tf_op jit(solution)/shard_map/dot_general | solution.py:14
  63.8 2.8 all-gather.5.cloned.1.call-done
  66.6 11.4 %fusion.90 = f32[256,3584]{1,0:T(8,128)} fusion(bf16[256,2048]{1,0:T(8,128)(2,1)} %all-gather.5.cloned.1.call-done, bf16[3584,2048]{1,0:T(8,128)(2,1)} %param.23), kind=kOutput, calls=%fused_computation.128 | convolution fusion | flops 3758096384 | bytes 19398656 | tf_op jit(solution)/shard_map/dot_general | solution.py:18
  78.0 7.5 %pad_maximum_fusion = f32[256,10752]{1,0:T(8,128)} fusion(f32[256,3584]{1,0:T(8,128)} %fusion.90, f32[256,3584]{1,0:T(8,128)} %fusion.89, f32[256,3584]{1,0:T(8,128)S(1)} %copy-done.17), kind=kLoop, calls=%fused_computation | loop fusion | flops 5505024 | bytes 22020096 | tf_op jit(solution)/shard_map/concatenate | solution.py:125
  85.6 0.0 all-reduce.4.cloned.1.call-update
  85.6 0.0 all-reduce.6.cloned.1.call-start
  85.7 1.1 copy-done.26
  86.8 1.5 convolution_bitcast_fusion
  88.4 1.5 fusion.38
  89.9 35.4 %all-reduce.7 = bf16[256,384]{0,1:T(8,128)(2,1)S(1)} all-reduce(f32[256,384]{0,1:T(8,128)S(1)} %pad_maximum_fusion.2), channel_id=1, replica_groups=mesh['row'=4,'col'=8] {'row'}, use_global_device_ids=true, to_apply=%region_3.0 | all-reduce | flops 98304 | bytes 589824 | tf_op jit(solution)/shard_map/psum | solution.py:123
  125.3 0.7 fusion.57
  126.0 0.7 fusion.64
  126.6 2.5 fusion.61
  129.1 2.5 fusion
  131.6 2.5 fusion.2
  134.1 178.0 %all-reduce.4.cloned.1.call-done = f32[256,10752]{1,0:T(8,128)} async-done(((f32[256,10752]{1,0:T(8,128)}), f32[256,10752]{1,0:T(8,128)}) %all-reduce.4.cloned.1.call-update) | async-done | bytes 11010064 | tf_op jit(solution)/shard_map/psum | solution.py:124
  312.1 4.5 fusion.3
  316.6 4.7 %fusion.5 = f32[256,3584]{1,0:T(8,128)} fusion(bf16[3584,64]{0,1:T(8,128)(2,1)S(1)} %copy-done.12, f32[256,10752]{1,0:T(8,128)} %all-reduce.4.cloned.1.call-done, bf16[256,384]{0,1:T(8,128)(2,1)S(1)} %all-reduce.7), kind=kOutput, calls=%fused_computation.12 | convolution fusion | flops 119275520 | bytes 7831552 | tf_op jit(solution)/shard_map/dot_general | solution.py:18
  321.3 4.7 %fusion.4 = f32[256,3584]{1,0:T(8,128)} fusion(bf16[64,3584]{1,0:T(8,128)(2,1)S(1)} %copy-done.9, f32[256,10752]{1,0:T(8,128)} %all-reduce.4.cloned.1.call-done, bf16[256,384]{0,1:T(8,128)(2,1)S(1)} %all-reduce.7), kind=kOutput, calls=%fused_computation.10 | convolution fusion | flops 119275520 | bytes 7831552 | tf_op jit(solution)/shard_map/dot_general | solution.py:14
  326.1 0.5 copy-done.15
  326.5 9.5 %add_convert_fusion = (bf16[256,3584]{1,0:T(8,128)(2,1)}, bf16[256,3584]{1,0:T(8,128)(2,1)S(1)}, bf16[256,3584]{1,0:T(8,128)(2,1)}, bf16[256,3584]{1,0:T(8,128)(...) fusion(f32[256,3584]{1,0:T(8,128)} %fusion.4, f32[256,3584]{1,0:T(8,128)S(1)} %copy-done.15, ...), kind=kOutput, calls=%fused_computation.31 | convolution fusion | flops 155975680 | bytes 33521664 | tf_op jit(solution)/shard_map/dot_general | solution.py:14
  336.1 1.9 fusion.29
  337.9 8.6 %fusion.91 = f32[256,2048]{1,0:T(8,128)} fusion(bf16[256,3584]{1,0:T(8,128)(2,1)S(1)} %get-tuple-element.11, bf16[2048,3584]{1,0:T(8,128)(2,1)} %param.21), kind=kOutput, calls=%fused_computation.129 | convolution fusion | flops 3758096384 | bytes 18612224 | tf_op jit(solution)/shard_map/dot_general | solution.py:18
  346.5 0.7 fusion.93
  347.2 8.7 %fusion.92 = f32[256,2048]{1,0:T(8,128)} fusion(bf16[256,3584]{1,0:T(8,128)(2,1)S(1)} %get-tuple-element.9, bf16[2048,3584]{1,0:T(8,128)(2,1)} %param.21), kind=kOutput, calls=%fused_computation.130 | convolution fusion | flops 3758096384 | bytes 18612224 | tf_op jit(solution)/shard_map/dot_general | solution.py:18
  355.9 2.2 fusion.94
  358.1 2.2 fusion.95
  360.3 1.3 fusion.31
  361.6 1.3 fusion.37
  362.9 1.3 fusion.35
  364.2 1.3 fusion.33
  365.5 0.3 reduce-scatter.2.cloned.1.call-start
  365.8 10.3 %fusion.19 = bf16[256,2048]{1,0:T(8,128)(2,1)S(1)} fusion(f32[256,2048]{1,0:T(8,128)} %fusion.91, bf16[256,3584]{1,0:T(8,128)(2,1)} %copy-done.1, bf16[2048,3584]{1,0:T(8,128)(2,1)} %param.22), kind=kOutput, calls=%fused_computation.39 | convolution fusion | flops 3759144960 | bytes 19660800 | tf_op jit(solution)/shard_map/dot_general | solution.py:18
  376.1 11.3 %fusion.20 = bf16[256,2048]{1,0:T(8,128)(2,1)} fusion(f32[256,2048]{1,0:T(8,128)} %fusion.92, bf16[256,3584]{1,0:T(8,128)(2,1)} %get-tuple-element.10, bf16[2048,3584]{1,0:T(8,128)(2,1)} %param.22), kind=kOutput, calls=%fused_computation.40 | convolution fusion | flops 3759144960 | bytes 19660800 | tf_op jit(solution)/shard_map/dot_general | solution.py:18
  387.4 2.8 pad_maximum_fusion.1
  390.2 0.0 reduce-scatter.2.cloned.1.call-update
  390.3 2.1 fusion.72
  392.4 0.4 fusion.59
  392.8 0.4 fusion.55
  393.3 1.4 fusion.6
  394.6 1.4 fusion.7
  396.0 1.4 fusion.8
  397.4 20.9 %all-reduce.6.cloned.1.call-done = bf16[320,256]{1,0:T(8,128)(2,1)} async-done(((bf16[320,256]{1,0:T(8,128)(2,1)}), bf16[320,256]{1,0:T(8,128)(2,1)}) %all-reduce.6.cloned.1.call-update) | async-done | bytes 163856 | tf_op jit(solution)/shard_map/psum | solution.py:227
  418.3 1.1 fusion.80
  419.4 1.0 fusion.77
  420.4 1.3 convolution_add_fusion.10
  421.7 1.0 convolution_add_fusion.9
  422.7 1.9 convolution_multiply_fusion.3
  424.6 1.1 convolution_multiply_fusion.4
  425.7 1.1 convolution_multiply_fusion.5
  426.8 31.5 %reduce-scatter.2.cloned.1.call-done = bf16[32,4096]{1,0:T(8,128)(2,1)} async-done(((bf16[256,4096]{1,0:T(8,128)(2,1)}), bf16[32,4096]{1,0:T(8,128)(2,1)}) %reduce-scatter.2.cloned.1.call-update) | async-done | bytes 262160 | tf_op jit(solution)/shard_map/reduce_scatter | solution.py:235
  458.2 1.0 convert_element_type.46
  459.2 2.0 fusion.22
  461.1 1.0 fusion.24
  (61 shorter events, 0.2 us)
Async XLA Ops:
  7.2 318.9 %copy-start = (bf16[64,3584]{1,0:T(8,128)(2,1)S(1)}, bf16[64,3584]{1,0:T(8,128)(2,1)}, u32[]{:S(2)}) copy-start(bf16[64,3584]{1,0:T(8,128)(2,1)} %param.33) | copy-start | bytes 1376260
  7.2 36.0 %all-gather.3.cloned.1.call-start = ((), (), s32[]{:S(2)}) async-start(), calls=%async_computation.1 | async-start | bytes 1179648 | tf_op jit(solution)/shard_map/all_gather | solution.py:106
  21.4 45.2 %all-gather.5.cloned.1.call-start = ((), (), s32[]{:S(2)}) async-start(), calls=%async_computation.2 | async-start | bytes 1179648 | tf_op jit(solution)/shard_map/all_gather | solution.py:107
  22.1 289.9 %all-reduce.4.cloned.1.call-start = ((), (), s32[]{:S(2)}) async-start(), calls=%async_computation.3 | async-start | bytes 22020096 | tf_op jit(solution)/shard_map/psum | solution.py:124
  43.2 11.5 %copy-start.10 = (bf16[256,2048]{1,0:T(8,128)(2,1)S(1)}, bf16[256,2048]{1,0:T(8,128)(2,1)}, u32[]{:S(2)}) copy-start(bf16[256,2048]{1,0:T(8,128)(2,1)} %all-gather.3.cloned.1.call-done) | copy-start | bytes 3145732
  66.6 11.4 %copy-start.17 = (f32[256,3584]{1,0:T(8,128)S(1)}, f32[256,3584]{1,0:T(8,128)}, u32[]{:S(2)}) copy-start(f32[256,3584]{1,0:T(8,128)} %fusion.88) | copy-start | bytes 11010052
  85.6 1.2 copy-start.26
  85.6 2.7 copy-start.22
  85.6 2.8 copy-start.24
  85.6 2.8 copy-start.28
  85.6 332.7 %all-reduce.6.cloned.1.call-start = ((), (), s32[]{:S(2)}) async-start(), calls=%async_computation.5 | async-start | bytes 327680 | tf_op jit(solution)/shard_map/psum | solution.py:227
  88.3 36.9 %copy-start.8 = (bf16[64,3584]{1,0:T(8,128)(2,1)S(1)}, bf16[64,3584]{1,0:T(8,128)(2,1)}, u32[]{:S(2)}) copy-start(bf16[64,3584]{1,0:T(8,128)(2,1)} %param.25) | copy-start | bytes 1376260
  89.8 36.1 %copy-start.12 = (bf16[3584,64]{0,1:T(8,128)(2,1)S(1)}, bf16[3584,64]{0,1:T(8,128)(2,1)}, u32[]{:S(2)}) copy-start(bf16[3584,64]{0,1:T(8,128)(2,1)} %param.28) | copy-start | bytes 1376260
  125.3 1.4 copy-start.9
  126.0 3.2 copy-start.18
  129.1 2.5 copy-start.20
  316.6 9.5 %copy-start.16 = (f32[256,3584]{1,0:T(8,128)S(1)}, f32[256,3584]{1,0:T(8,128)}, u32[]{:S(2)}) copy-start(f32[256,3584]{1,0:T(8,128)} %fusion.2) | copy-start | bytes 11010052
  321.3 4.7 %copy-start.14 = (f32[256,3584]{1,0:T(8,128)S(1)}, f32[256,3584]{1,0:T(8,128)}, u32[]{:S(2)}) copy-start(f32[256,3584]{1,0:T(8,128)} %fusion.61) | copy-start | bytes 11010052
  321.3 5.2 %copy-start.15 = (f32[256,3584]{1,0:T(8,128)S(1)}, f32[256,3584]{1,0:T(8,128)}, u32[]{:S(2)}) copy-start(f32[256,3584]{1,0:T(8,128)} %fusion) | copy-start | bytes 11010052
  336.1 11.2 %copy-start.3 = (bf16[256,3584]{1,0:T(8,128)(2,1)}, bf16[256,3584]{1,0:T(8,128)(2,1)S(1)}, u32[]{:S(2)}) copy-start(bf16[256,3584]{1,0:T(8,128)(2,1)S(1)} %get-tuple-element.9) | copy-start | bytes 5505028
  336.1 26.9 %copy-start.1 = (bf16[256,3584]{1,0:T(8,128)(2,1)}, bf16[256,3584]{1,0:T(8,128)(2,1)S(1)}, u32[]{:S(2)}) copy-start(bf16[256,3584]{1,0:T(8,128)(2,1)S(1)} %get-tuple-element.12) | copy-start | bytes 5505028
  347.2 10.9 %copy-start.13 = (bf16[3584,64]{0,1:T(8,128)(2,1)S(1)}, bf16[3584,64]{0,1:T(8,128)(2,1)}, u32[]{:S(2)}) copy-start(bf16[3584,64]{0,1:T(8,128)(2,1)} %param.28) | copy-start | bytes 1376260
  355.9 5.7 %copy-start.19 = (bf16[64,3584]{1,0:T(8,128)(2,1)S(1)}, bf16[64,3584]{1,0:T(8,128)(2,1)}, u32[]{:S(2)}) copy-start(bf16[64,3584]{1,0:T(8,128)(2,1)} %param.31) | copy-start | bytes 1376260
  360.3 3.9 copy-start.6
  360.3 3.9 copy-start.21
  365.5 92.7 %reduce-scatter.2.cloned.1.call-start = ((), (), s32[]{:S(2)}) async-start(), calls=%async_computation.4 | async-start | bytes 2359296 | tf_op jit(solution)/shard_map/reduce_scatter | solution.py:235
  390.2 2.1 copy-start.2
  390.2 3.0 copy-start.7
  392.8 1.8 copy-start.5
  393.3 2.8 copy-start.4
  394.6 23.7 %copy-start.25 = (bf16[2048,64]{0,1:T(8,128)(2,1)S(1)}, bf16[2048,64]{0,1:T(8,128)(2,1)}, u32[]{:S(2)}) copy-start(bf16[2048,64]{0,1:T(8,128)(2,1)} %param.24) | copy-start | bytes 786436
  396.0 25.6 %copy-start.23 = (bf16[2048,64]{0,1:T(8,128)(2,1)S(1)}, bf16[2048,64]{0,1:T(8,128)(2,1)}, u32[]{:S(2)}) copy-start(bf16[2048,64]{0,1:T(8,128)(2,1)} %param.26) | copy-start | bytes 786436
  396.0 26.7 %copy-start.11 = (bf16[256,2048]{1,0:T(8,128)(2,1)S(1)}, bf16[256,2048]{1,0:T(8,128)(2,1)}, u32[]{:S(2)}) copy-start(bf16[256,2048]{1,0:T(8,128)(2,1)} %all-gather.3.cloned.1.call-done) | copy-start | bytes 3145732
  397.4 28.2 %copy-start.27 = (bf16[256,2048]{1,0:T(8,128)(2,1)S(1)}, bf16[256,2048]{1,0:T(8,128)(2,1)}, u32[]{:S(2)}) copy-start(bf16[256,2048]{1,0:T(8,128)(2,1)} %all-gather.5.cloned.1.call-done) | copy-start | bytes 3145732
  418.3 6.2 %copy-start.29 = (bf16[320,256]{1,0:T(8,128)(2,1)S(1)}, bf16[320,256]{1,0:T(8,128)(2,1)}, u32[]{:S(2)}) copy-start(bf16[320,256]{1,0:T(8,128)(2,1)} %all-reduce.6.cloned.1.call-done) | copy-start | bytes 491524
Sparse Core Ops, SparseCore 0:
  21.5 21.6 all-gather.2
  44.8 21.8 all-gather.4
  85.7 226.3 all-reduce.3
  365.7 52.6 all-reduce.5
  420.5 37.6 reduce-scatter.1
where the time goes:
time: 469 us
  waiting for transfers between devices  255 us (54%)
  matrix products  137 us (29%)
  blocking collectives  46.8 us (10%)
  other arithmetic  14.1 us (3%)
  between operations  14.1 us (3%)
    psum x1, waiting for transfers between devices, on_device(): lax.psum(jnp.concatenate([curvature_product(normed_tokens, gate_frozen_we...  178 us
    dot_general x15, matrix products, cross_shard_total(): lax.dot_general(left, right, (((1,), (1,)), ((), ())), preferred_element_...  68.3 us
    dot_general x9, matrix products, curvature_product(): return jnp.dot(left, right, preferred_element_type=jnp.float32)  46.5 us
    psum x1, blocking collectives, on_device(): ranks = lax.psum(projected, 'row').astype(jnp.bfloat16)  35.4 us
    reduce_scatter x1, waiting for transfers between devices, on_device(): lax.psum_scatter(jnp.concatenate([adjoint_contribution, tangent_contribut...  31.5 us
    all_gather x1, waiting for transfers between devices, on_device(): lax.all_gather(own_normed, 'col', axis=0, tiled=True)  21 us
    psum x1, waiting for transfers between devices, on_device(): lax.psum(rank_adjoints.astype(jnp.bfloat16), 'col').astype(jnp.float32)  20.9 us
    psum x1, blocking collectives, on_device(): squares = lax.psum(jnp.sum(tokens_f * tokens_f, axis=1), 'row')  11.4 us
  transfers between devices with their start and end apart: 5, of which 5 were waited for; matrix products, arithmetic and copies ran while one was open for 15% of the time, Pallas kernels for 0%

commit v1 on v0

v1 whole, which is shorter than its diff:
```python
import functools

import jax
import jax.numpy as jnp
from jax import lax
from jax.experimental import pallas as pl
from jax.experimental.pallas import tpu as pltpu
from jax.sharding import PartitionSpec as P

adapter_scale = 0.5
epsilon = 1e-05
MESH = pl.DeviceIdType.MESH


def total_kernel(axis, n, x_ref, o_ref, inbox, whole, send1, recv1, send2, recv2):
    me = lax.axis_index(axis)
    barrier = pltpu.get_barrier_semaphore()

    @pl.loop(1, n)
    def _(k):
        pl.semaphore_signal(
            barrier, inc=1, device_id={axis: lax.rem(me + k, n)}, device_id_type=MESH
        )

    pl.semaphore_wait(barrier, n - 1)

    def scatter(k):
        peer = lax.rem(me + k, n)
        return pltpu.make_async_remote_copy(
            src_ref=x_ref.at[peer],
            dst_ref=inbox.at[k],
            send_sem=send1.at[k],
            recv_sem=recv1.at[k],
            device_id={axis: peer},
            device_id_type=MESH,
        )

    def spread(k):
        peer = lax.rem(me + k, n)
        return pltpu.make_async_remote_copy(
            src_ref=whole.at[me],
            dst_ref=whole.at[me],
            send_sem=send2.at[k],
            recv_sem=recv2.at[k],
            device_id={axis: peer},
            device_id_type=MESH,
        )

    def arrival(k):
        origin = lax.rem(me - k + n, n)
        return pltpu.make_async_remote_copy(
            src_ref=whole.at[origin],
            dst_ref=whole.at[origin],
            send_sem=send2.at[k],
            recv_sem=recv2.at[k],
            device_id={axis: origin},
            device_id_type=MESH,
        )

    @pl.loop(1, n)
    def _(k):
        scatter(k).start()

    def add(k, total):
        scatter(k).wait_recv()
        return total + inbox[k].astype(jnp.float32)

    total = lax.fori_loop(1, n, add, x_ref[me].astype(jnp.float32))
    whole[me] = total.astype(whole.dtype)

    @pl.loop(1, n)
    def _(k):
        spread(k).start()

    @pl.loop(1, n)
    def _(k):
        arrival(k).wait_recv()

    @pl.loop(1, n)
    def _(k):
        scatter(k).wait_send()
        spread(k).wait_send()

    o_ref[...] = whole[...]


def shard_total(x, axis, collective_id):
    n = lax.axis_size(axis)
    rows, columns = x.shape
    block = (n, rows // n, columns)
    total = pl.pallas_call(
        functools.partial(total_kernel, axis, n),
        out_shape=jax.ShapeDtypeStruct(block, jnp.bfloat16),
        in_specs=[pl.BlockSpec(memory_space=pltpu.VMEM)],
        out_specs=pl.BlockSpec(memory_space=pltpu.VMEM),
        scratch_shapes=[
            pltpu.VMEM(block, x.dtype),
            pltpu.VMEM(block, jnp.bfloat16),
            pltpu.SemaphoreType.DMA((n,)),
            pltpu.SemaphoreType.DMA((n,)),
            pltpu.SemaphoreType.DMA((n,)),
            pltpu.SemaphoreType.DMA((n,)),
        ],
        compiler_params=pltpu.CompilerParams(collective_id=collective_id, has_side_effects=True),
        name=f"total_{axis}",
    )(x.reshape(block))
    return total.reshape(rows, columns)


def curvature_product(left, right):
    return jnp.dot(left, right, preferred_element_type=jnp.float32)


def cross_shard_total(left, right):
    return lax.dot_general(
        left, right, (((1,), (1,)), ((), ())), preferred_element_type=jnp.float32
    )


def summed_over_rows(left, right):
    return lax.dot_general(
        left, right, (((0,), (0,)), ((), ())), preferred_element_type=jnp.float32
    )


def second_order(
    gate_preactivation,
    up_preactivation,
    hidden_adjoint,
    gate_tangent_rows,
    up_tangent_rows,
    adjoint_tangent_rows,
):
    sigma = jax.nn.sigmoid(gate_preactivation)
    silu_value = gate_preactivation * sigma
    slope = sigma * (1.0 + gate_preactivation * (1.0 - sigma))
    bend = sigma * (1.0 - sigma) * (2.0 + gate_preactivation * (1.0 - 2.0 * sigma))
    hidden_activation = (silu_value * up_preactivation).astype(jnp.bfloat16)
    hidden_direction = (
        slope * gate_tangent_rows * up_preactivation + silu_value * up_tangent_rows
    ).astype(jnp.bfloat16)
    gate_derivative = (hidden_adjoint * up_preactivation * slope).astype(jnp.bfloat16)
    up_derivative = (hidden_adjoint * silu_value).astype(jnp.bfloat16)
    gate_derivative_direction = (
        adjoint_tangent_rows * up_preactivation * slope
        + hidden_adjoint * (up_tangent_rows * slope + up_preactivation * bend * gate_tangent_rows)
    ).astype(jnp.bfloat16)
    up_derivative_direction = (
        adjoint_tangent_rows * silu_value + hidden_adjoint * slope * gate_tangent_rows
    ).astype(jnp.bfloat16)
    return (
        hidden_activation,
        hidden_direction,
        gate_derivative,
        up_derivative,
        gate_derivative_direction,
        up_derivative_direction,
    )


def chunk_count(width):
    for count in (4, 2):
        if width % (128 * count) == 0:
            return count
    return 1


def on_device(
    tokens,
    norm_gain,
    cotangent,
    gate_frozen_weight,
    up_frozen_weight,
    down_frozen_weight,
    gate_input_factor,
    gate_output_factor,
    up_input_factor,
    up_output_factor,
    down_input_factor,
    down_b,
    gate_input_factor_direction,
    gate_output_factor_direction,
    up_input_factor_direction,
    up_output_factor_direction,
    down_input_factor_direction,
    down_b_dir,
):
    rank = gate_input_factor.shape[1]
    width_rows, width_columns = gate_frozen_weight.shape
    features = width_rows * lax.axis_size("row")
    own_count = tokens.shape[0]
    cot_panel = lax.all_gather(cotangent, "col", axis=0, tiled=True)
    tokens_f = tokens.astype(jnp.float32)
    squares = lax.psum(jnp.sum(tokens_f * tokens_f, axis=1), "row")
    own_normed = (tokens_f * lax.rsqrt(squares[:, None] / features + epsilon) * norm_gain).astype(
        jnp.bfloat16
    )
    normed_tokens = lax.all_gather(own_normed, "col", axis=0, tiled=True)
    count = normed_tokens.shape[0]
    chunks = chunk_count(width_columns)
    wide = width_columns // chunks
    spans = [slice(index * wide, (index + 1) * wide) for index in range(chunks)]

    in_factors = jnp.concatenate(
        [
            gate_input_factor,
            up_input_factor,
            gate_input_factor_direction,
            up_input_factor_direction,
        ],
        axis=1,
    )
    out_factors = jnp.concatenate([down_b, down_b_dir], axis=0)

    summed_chunks = []
    for span in spans:
        partial = (
            curvature_product(normed_tokens, gate_frozen_weight[:, span]).astype(jnp.bfloat16),
            curvature_product(normed_tokens, up_frozen_weight[:, span]).astype(jnp.bfloat16),
            cross_shard_total(cot_panel, down_frozen_weight[span]).astype(jnp.bfloat16),
        )
        if summed_chunks:
            partial, summed_chunks[-1] = lax.optimization_barrier((partial, summed_chunks[-1]))
        summed_chunks.append(lax.psum(partial, "row"))

    projected = jnp.concatenate(
        [curvature_product(normed_tokens, in_factors), cross_shard_total(cot_panel, out_factors)],
        axis=1,
    )
    ranks = shard_total(projected, "row", 0)
    gate_low, up_low, gate_low_dir, up_low_dir, adj_low, adj_low_dir = [
        ranks[:, index * rank : (index + 1) * rank] for index in range(6)
    ]
    gate_pair = jnp.concatenate([gate_low_dir, gate_low], axis=1)
    up_pair = jnp.concatenate([up_low_dir, up_low], axis=1)
    adj_pair = jnp.concatenate([adj_low_dir, adj_low], axis=1)
    gate_stack = jnp.concatenate([gate_low_dir, gate_low], axis=0)
    up_stack = jnp.concatenate([up_low_dir, up_low], axis=0)
    adj_stack = jnp.concatenate([adj_low, adj_low_dir], axis=0)
    gate_out = jnp.concatenate([gate_output_factor, gate_output_factor_direction], axis=0)
    up_out = jnp.concatenate([up_output_factor, up_output_factor_direction], axis=0)
    down_in = jnp.concatenate([down_input_factor, down_input_factor_direction], axis=1)

    feature = 0.0
    gate_q = 0.0
    up_q = 0.0
    low_dir = 0.0
    gate_output, up_output, down_input = [], [], []
    for span, total in zip(spans, summed_chunks):
        gate_sum, up_sum, adj_sum = [value.astype(jnp.float32) for value in total]
        gate_pre = gate_sum + adapter_scale * curvature_product(
            gate_low, gate_output_factor[:, span]
        )
        up_pre = up_sum + adapter_scale * curvature_product(
            up_low, up_output_factor[:, span]
        )
        hidden_adj = adj_sum + adapter_scale * cross_shard_total(
            adj_low, down_input_factor[span]
        )
        gate_tan = adapter_scale * curvature_product(gate_pair, gate_out[:, span])
        up_tan = adapter_scale * curvature_product(up_pair, up_out[:, span])
        adj_tan = adapter_scale * cross_shard_total(adj_pair, down_in[span])
        hidden, hidden_dir, d_gate, d_up, d_gate_dir, d_up_dir = second_order(
            gate_pre, up_pre, hidden_adj, gate_tan, up_tan, adj_tan
        )
        gate_d = jnp.concatenate([d_gate, d_gate_dir], axis=0)
        up_d = jnp.concatenate([d_up, d_up_dir], axis=0)
        hidden_d = jnp.concatenate([hidden_dir, hidden], axis=0)
        gate_output.append(adapter_scale * summed_over_rows(gate_stack, gate_d))
        up_output.append(adapter_scale * summed_over_rows(up_stack, up_d))
        down_input.append(adapter_scale * summed_over_rows(hidden_d, adj_stack))
        gate_q = gate_q + cross_shard_total(gate_d, gate_out[:, span])
        up_q = up_q + cross_shard_total(up_d, up_out[:, span])
        low_dir = (
            low_dir
            + curvature_product(hidden_dir, down_input_factor[span])
            + curvature_product(hidden, down_input_factor_direction[span])
        )
        feature = (
            feature
            + cross_shard_total(gate_d, gate_frozen_weight[:, span])
            + cross_shard_total(up_d, up_frozen_weight[:, span])
        )

    summed = lax.psum_scatter(
        feature.astype(jnp.bfloat16).reshape(2, count, width_rows),
        "col",
        scatter_dimension=1,
        tiled=True,
    ).astype(jnp.float32)
    adjoints = shard_total(
        jnp.concatenate(
            [
                gate_q[:count, :rank],
                up_q[:count, :rank],
                gate_q[count:, :rank] + gate_q[:count, rank:],
                up_q[count:, :rank] + up_q[:count, rank:],
                low_dir,
            ],
            axis=1,
        ).astype(jnp.bfloat16),
        "col",
        1,
    )
    piece = lax.dynamic_slice_in_dim(adjoints, lax.axis_index("col") * own_count, own_count, 0)
    normed_feature_adjoint = summed[0] + adapter_scale * cross_shard_total(
        piece[:, : 2 * rank], in_factors[:, : 2 * rank]
    )
    normed_feature_adjoint_direction = summed[1] + adapter_scale * cross_shard_total(
        jnp.concatenate([piece[:, 2 * rank : 4 * rank], piece[:, : 2 * rank]], axis=1), in_factors
    )
    gate_input = adapter_scale * summed_over_rows(
        normed_tokens, adjoints[:, 2 * rank : 3 * rank]
    )
    up_input = adapter_scale * summed_over_rows(normed_tokens, adjoints[:, 3 * rank : 4 * rank])
    down_output = adapter_scale * summed_over_rows(adjoints[:, 4 * rank :], cot_panel)
    return (
        normed_feature_adjoint,
        normed_feature_adjoint_direction,
        gate_input,
        jnp.concatenate(gate_output, axis=1),
        up_input,
        jnp.concatenate(up_output, axis=1),
        jnp.concatenate(down_input, axis=0),
        down_output,
    )


def solution(mesh):
    in_specs = (
        P("col", "row"),
        P("row"),
        P("col", "row"),
        P("row", "col"),
        P("row", "col"),
        P("col", "row"),
        P("row", None),
        P(None, "col"),
        P("row", None),
        P(None, "col"),
        P("col", None),
        P(None, "row"),
        P("row", None),
        P(None, "col"),
        P("row", None),
        P(None, "col"),
        P("col", None),
        P(None, "row"),
    )
    out_specs = (
        P("col", "row"),
        P("col", "row"),
        P("row", None),
        P(None, "col"),
        P("row", None),
        P(None, "col"),
        P("col", None),
        P(None, "row"),
    )
    return jax.shard_map(
        on_device, mesh=mesh, in_specs=in_specs, out_specs=out_specs, check_vma=False
    )
```

time: 469 us -> 470 us (level); the launches traced: 469 us -> 461 us
  waiting for transfers between devices: 255 us -> 164 us
  matrix products: 137 us -> 203 us
  blocking collectives: 46.8 us -> 11.4 us
  Pallas kernels: 0 us -> 32.9 us
  local copies, waits for them, and re-layouts: 1.74 us -> 24.1 us
    psum x2 -> x4, waiting for transfers between devices: 199 us -> 132 us  [on_device(): summed_chunks.append(lax.psum(partial, 'row'))]
    dot_general x15 -> x31, matrix products: 68.3 us -> 105 us  [cross_shard_total(): lax.dot_general(left, right, (((1,), (1,)), ((), ())), preferred_element_...]
    psum x1 -> x0, blocking collectives: 35.4 us -> none  [on_device(): ranks = lax.psum(projected, 'row').astype(jnp.bfloat16)]
    pallas_call x0 -> x2, Pallas kernels: none -> 32.9 us  [shard_total(): pl.pallas_call(functools.partial(total_kernel, axis, n), out_shape=jax.Sh...]
    reduce_scatter x1, waiting for transfers between devices: 31.5 us -> 0.01 us  [on_device(): lax.psum_scatter(feature.astype(jnp.bfloat16).reshape(2, count, width_row...]
    dot_general x9 -> x33, matrix products: 46.5 us -> 74.3 us  [curvature_product(): return jnp.dot(left, right, preferred_element_type=jnp.float32)]
    dot_general x6 -> x15, matrix products: 7.12 us -> 24.4 us  [summed_over_rows(): lax.dot_general(left, right, (((0,), (0,)), ((), ())), preferred_element_...]
    dot_general x11 -> x0, matrix products: 14.8 us -> none  [the longest x6 7.28 us: lifted(): lax.dot_general(adjoint, factor, (((0,), (1,)), ((), ())), precision=lax....]
  transfers between devices with their start and end apart: 5 -> 7, of which waited for: 5 -> 6; matrix products, arithmetic and copies ran while one was open for 15% -> 30% of each run, Pallas kernels for 0% -> 4%
where the time goes in v1:
time: 470 us; the launch traced here: 461 us
  matrix products  203 us (43%)
  waiting for transfers between devices  164 us (35%)
  Pallas kernels  32.9 us (7%)
  local copies, waits for them, and re-layouts  24.1 us (5%)
  between operations  15.1 us (3%)
  blocking collectives  11.4 us (2%)
  other arithmetic  9.98 us (2%)
    psum x4, waiting for transfers between devices, on_device(): summed_chunks.append(lax.psum(partial, 'row'))  132 us
    dot_general x31, matrix products, cross_shard_total(): lax.dot_general(left, right, (((1,), (1,)), ((), ())), preferred_element_...  105 us
    dot_general x33, matrix products, curvature_product(): return jnp.dot(left, right, preferred_element_type=jnp.float32)  74.3 us
    pallas_call x2, Pallas kernels, shard_total(): pl.pallas_call(functools.partial(total_kernel, axis, n), out_shape=jax.Sh...  32.9 us
    dot_general x15, matrix products, summed_over_rows(): lax.dot_general(left, right, (((0,), (0,)), ((), ())), preferred_element_...  24.4 us
    all_gather x1, waiting for transfers between devices, on_device(): cot_panel = lax.all_gather(cotangent, 'col', axis=0, tiled=True)  21 us
    psum x1, blocking collectives, on_device(): squares = lax.psum(jnp.sum(tokens_f * tokens_f, axis=1), 'row')  11.4 us
    all_gather x1, waiting for transfers between devices, on_device(): normed_tokens = lax.all_gather(own_normed, 'col', axis=0, tiled=True)  9.85 us
  transfers between devices with their start and end apart: 7, of which 6 were waited for; matrix products, arithmetic and copies ran while one was open for 30% of the time, Pallas kernels for 4%

profile of v1, /device:TPU:0, one launch (start us, length us, event | category | flops | bytes accessed | tf_op | source)
XLA Modules:
  0.0 461.3 jit_solution(9519683693839613962)
XLA Ops:
  8.3 11.4 %psum.91 = f32[32]{0:T(128)S(1)} all-reduce(f32[32]{0:T(128)S(1)} %fusion.153), channel_id=1, replica_groups=mesh['row'=4,'col'=8] {'row'}, use_global_device_ids=true, to_apply=%region_1.0 | all-reduce | flops 32 | bytes 256 | tf_op jit(solution)/shard_map/psum | solution.py:194
  19.7 1.7 fusion.155
  23.2 1.8 constant_dynamic-update-slice_fusion.7
  31.1 2.2 constant_dynamic-update-slice_fusion.6
  33.3 9.9 %all-gather.3.cloned.1.call-done = bf16[256,2048]{1,0:T(8,128)(2,1)} async-done(((bf16[32,2048]{1,0:T(8,128)(2,1)}), bf16[256,2048]{1,0:T(8,128)(2,1)}) %all-gather.3.cloned.1.call-update) | async-done | bytes 1048592 | tf_op jit(solution)/shard_map/all_gather | solution.py:198
  43.2 2.4 fusion.250
  45.6 21.0 %all-gather.5.cloned.1.call-done = bf16[256,2048]{1,0:T(8,128)(2,1)} async-done(((bf16[32,2048]{1,0:T(8,128)(2,1)}), bf16[256,2048]{1,0:T(8,128)(2,1)}) %all-gather.5.cloned.1.call-update) | async-done | bytes 1048592 | tf_op jit(solution)/shard_map/all_gather | solution.py:192
  66.6 1.9 convolution_bitcast_fusion
  70.4 14.3 %total_row.1 = bf16[4,64,384]{2,1,0:T(8,128)(2,1)} custom-call(f32[4,64,384]{2,1,0:T(8,128)} %bitcast.73), custom_call_target="tpu_custom_call" | custom-call | tf_op jit(solution)/shard_map/total_row/pallas_call | solution.py:91
  95.2 4.1 fusion.65
  99.3 4.1 fusion.62
  103.5 4.1 fusion.83
  107.8 4.1 fusion.77
  111.9 4.1 fusion.74
  115.9 4.2 fusion.71
  120.1 4.2 fusion.68
  124.3 4.1 fusion.59
  128.3 4.1 fusion.56
  132.4 2.1 convolution_multiply_fusion.23
  134.5 4.1 fusion.89
  138.6 4.2 fusion.86
  142.8 4.5 fusion.80
  147.3 16.6 %all-reduce.15.cloned.1.call-done = (bf16[256,896]{1,0:T(8,128)(2,1)}, bf16[256,896]{1,0:T(8,128)(2,1)}, bf16[256,896]{1,0:T(8,128)(2,1)}) async-done(((bf16[256,896]{1,0:T(8,128)(2,1)}, bf16[256,896]{1,0:T(8,128)(2,1)}, bf16[256,896]{1,0:T(8,128)(2,1)}), (bf16[256,896]{1,0:T(8,128)(2,1)}, bf16[256,896]{1,0:T(8,128)(2,1)}, bf16[256,896]{1,0:T(8,128)(2,1)})) %all-reduce.15.cloned.1.call-update) | async-done | bytes 1376272 | tf_op jit(solution)/shard_map/psum | solution.py:224
  168.2 2.1 add_convert_fusion.4
  171.6 2.3 fusion.152
  176.0 2.2 convolution_multiply_fusion.36
  178.2 2.2 convolution_multiply_fusion.32
  180.3 2.0 convolution_add_fusion.12
  182.4 6.5 %fusion.24 = f32[512,2048]{1,0:T(8,128)} fusion(bf16[2048,3584]{1,0:T(8,128)(2,1)} %param.22, bf16[256,896]{1,0:T(8,128)(2,1)S(1)} %copy-done.66, bf16[256,896]{1,0:T(8,128)(2,1)S(1)} %copy-done.68), kind=kOutput, calls=%fused_computation.25 | convolution fusion | flops 1880883200 | bytes 8781824 | tf_op jit(solution)/shard_map/dot_general | solution.py:115
  188.9 6.4 %fusion.28 = f32[512,2048]{1,0:T(8,128)} fusion(bf16[2048,3584]{1,0:T(8,128)(2,1)} %param.21, bf16[256,896]{1,0:T(8,128)(2,1)S(1)} %copy-done.62, bf16[256,896]{1,0:T(8,128)(2,1)S(1)} %copy-done.64), kind=kOutput, calls=%fused_computation.29 | convolution fusion | flops 1880883200 | bytes 8781824 | tf_op jit(solution)/shard_map/dot_general | solution.py:115
  195.3 38.3 %all-reduce.13.cloned.1.call-done = (bf16[256,896]{1,0:T(8,128)(2,1)}, bf16[256,896]{1,0:T(8,128)(2,1)}, bf16[256,896]{1,0:T(8,128)(2,1)}) async-done(((bf16[256,896]{1,0:T(8,128)(2,1)}, bf16[256,896]{1,0:T(8,128)(2,1)}, bf16[256,896]{1,0:T(8,128)(2,1)}), (bf16[256,896]{1,0:T(8,128)(2,1)}, bf16[256,896]{1,0:T(8,128)(2,1)}, bf16[256,896]{1,0:T(8,128)(2,1)})) %all-reduce.13.cloned.1.call-update) | async-done | bytes 1376272 | tf_op jit(solution)/shard_map/psum | solution.py:224
  233.6 1.5 fusion.51
  237.8 3.5 add_convert_fusion.3
  244.2 2.3 convolution_multiply_fusion.39
  246.5 2.2 convolution_multiply_fusion.35
  248.6 2.1 convolution_add_fusion.10
  250.7 2.1 convolution_add_fusion.5
  252.8 2.1 convolution_add_fusion.2
  254.9 6.5 %fusion.32 = f32[512,2048]{1,0:T(8,128)} fusion(bf16[2048,3584]{1,0:T(8,128)(2,1)} %param.22, bf16[256,896]{1,0:T(8,128)(2,1)S(1)} %copy-done.57, bf16[256,896]{1,0:T(8,128)(2,1)S(1)} %copy-done.58), kind=kOutput, calls=%fused_computation.33 | convolution fusion | flops 1880883200 | bytes 8781824 | tf_op jit(solution)/shard_map/dot_general | solution.py:115
  261.4 40.4 %all-reduce.11.cloned.1.call-done = (bf16[256,896]{1,0:T(8,128)(2,1)}, bf16[256,896]{1,0:T(8,128)(2,1)}, bf16[256,896]{1,0:T(8,128)(2,1)}) async-done(((bf16[256,896]{1,0:T(8,128)(2,1)}, bf16[256,896]{1,0:T(8,128)(2,1)}, bf16[256,896]{1,0:T(8,128)(2,1)}), (bf16[256,896]{1,0:T(8,128)(2,1)}, bf16[256,896]{1,0:T(8,128)(2,1)}, bf16[256,896]{1,0:T(8,128)(2,1)})) %all-reduce.11.cloned.1.call-update) | async-done | bytes 1376272 | tf_op jit(solution)/shard_map/psum | solution.py:224
  301.8 1.5 fusion.48
  305.9 3.5 add_convert_fusion.2
  310.6 1.8 convolution_add_fusion.8
  312.9 2.6 convolution_add_fusion.4
  315.5 2.2 convolution_multiply_fusion.30
  318.6 2.1 convolution_add_fusion.1
  320.7 6.4 %fusion.16 = f32[512,2048]{1,0:T(8,128)} fusion(bf16[2048,3584]{1,0:T(8,128)(2,1)} %param.22, bf16[256,896]{1,0:T(8,128)(2,1)S(1)} %copy-done.51, bf16[256,896]{1,0:T(8,128)(2,1)S(1)} %copy-done.52), kind=kOutput, calls=%fused_computation.17 | convolution fusion | flops 1880883200 | bytes 8781824 | tf_op jit(solution)/shard_map/dot_general | solution.py:115
  327.1 6.5 %fusion.20 = f32[512,2048]{1,0:T(8,128)} fusion(bf16[2048,3584]{1,0:T(8,128)(2,1)} %param.21, bf16[256,896]{1,0:T(8,128)(2,1)S(1)} %copy-done.59, bf16[256,896]{1,0:T(8,128)(2,1)S(1)} %copy-done.60), kind=kOutput, calls=%fused_computation.21 | convolution fusion | flops 1880883200 | bytes 8781824 | tf_op jit(solution)/shard_map/dot_general | solution.py:115
  333.6 36.6 %all-reduce.9.cloned.1.call-done = (bf16[256,896]{1,0:T(8,128)(2,1)}, bf16[256,896]{1,0:T(8,128)(2,1)}, bf16[256,896]{1,0:T(8,128)(2,1)}) async-done(((bf16[256,896]{1,0:T(8,128)(2,1)}, bf16[256,896]{1,0:T(8,128)(2,1)}, bf16[256,896]{1,0:T(8,128)(2,1)}), (bf16[256,896]{1,0:T(8,128)(2,1)}, bf16[256,896]{1,0:T(8,128)(2,1)}, bf16[256,896]{1,0:T(8,128)(2,1)})) %all-reduce.9.cloned.1.call-update) | async-done | bytes 1376272 | tf_op jit(solution)/shard_map/psum | solution.py:224
  370.1 1.5 fusion.45
  374.3 3.2 add_convert_fusion.1
  377.5 7.1 %fusion.8 = f32[512,2048]{1,0:T(8,128)} fusion(bf16[2048,3584]{1,0:T(8,128)(2,1)} %param.22, bf16[256,896]{1,0:T(8,128)(2,1)S(1)} %get-tuple-element.58, bf16[256,896]{1,0:T(8,128)(2,1)S(1)} %get-tuple-element.72), kind=kOutput, calls=%fused_computation.9 | convolution fusion | flops 1880883200 | bytes 8781824 | tf_op jit(solution)/shard_map/dot_general | solution.py:115
  384.6 6.7 %fusion.12 = f32[512,2048]{1,0:T(8,128)} fusion(bf16[2048,3584]{1,0:T(8,128)(2,1)} %param.21, bf16[256,896]{1,0:T(8,128)(2,1)S(1)} %get-tuple-element.57, bf16[256,896]{1,0:T(8,128)(2,1)S(1)} %get-tuple-element.71), kind=kOutput, calls=%fused_computation.13 | convolution fusion | flops 1880883200 | bytes 8781824 | tf_op jit(solution)/shard_map/dot_general | solution.py:115
  391.3 12.5 %add_convert_fusion = bf16[512,2048]{1,0:T(8,128)(2,1)} fusion(f32[512,2048]{1,0:T(8,128)} %fusion.8, f32[512,2048]{1,0:T(8,128)} %fusion.12, f32[512,2048]{1,0:T(8,128)} %fusion.16, f32[512,2048]{1,0:T(8,128)} %fusion.20, f32[512,2048]{1,0:T(8,128)} %fusion.32, f32[512,2048]{1,0:T(8,128)} %fusion.28, f32[512,2048]{1,0:T(8,128)S(1)} %copy-done.2, ...), kind=kOutput, calls=%fused_computation | convolution fusion | flops 1889271808 | bytes 36044800 | tf_op jit(solution)/shard_map/dot_general | solution.py:115
  403.8 2.2 convolution_multiply_fusion.34
  408.4 1.7 convolution_add_fusion.3
  411.6 1.7 convolution_add_fusion
  414.7 1.5 copy.28
  416.2 1.5 fusion.200
  417.7 1.5 copy.30
  419.2 1.8 concatenate.124.x_ref
  420.9 18.6 %total_col.1 = bf16[8,32,320]{2,1,0:T(8,128)(2,1)} custom-call(bf16[8,32,320]{2,1,0:T(8,128)(2,1)} %concatenate.124.x_ref), custom_call_target="tpu_custom_call" | custom-call | tf_op jit(solution)/shard_map/total_col/pallas_call | solution.py:91
  440.3 1.5 convolution_multiply_fusion.29
  441.8 1.5 convolution_multiply_fusion.37
  (216 shorter events, 59.2 us)
Async XLA Ops:
  7.2 26.1 %copy-start.7 = (bf16[3584,64]{0,1:T(8,128)(2,1)S(1)}, bf16[3584,64]{0,1:T(8,128)(2,1)}, u32[]{:S(2)}) copy-start(bf16[3584,64]{0,1:T(8,128)(2,1)} %param.34) | copy-start | bytes 1376260
  7.2 36.0 %all-gather.3.cloned.1.call-start = ((), (), s32[]{:S(2)}) async-start(), calls=%async_computation.1 | async-start | bytes 1179648 | tf_op jit(solution)/shard_map/all_gather | solution.py:198
  21.4 45.2 %all-gather.5.cloned.1.call-start = ((), (), s32[]{:S(2)}) async-start(), calls=%async_computation.2 | async-start | bytes 1179648 | tf_op jit(solution)/shard_map/all_gather | solution.py:192
  22.1 141.8 %all-reduce.15.cloned.1.call-start = ((), (), s32[]{:S(2)}) async-start(), calls=%async_computation.7 | async-start | bytes 2752512 | tf_op jit(solution)/shard_map/psum | solution.py:224
  31.1 39.3 %copy-start.4 = (bf16[128,3584]{1,0:T(8,128)(2,1)}, bf16[128,3584]{1,0:T(8,128)(2,1)S(1)}, u32[]{:S(2)}) copy-start(bf16[128,3584]{1,0:T(8,128)(2,1)S(1)} %constant_dynamic-update-slice_fusion.8) | copy-start | bytes 2752516
  84.7 6.8 %copy-start.5 = (bf16[128,3584]{1,0:T(8,128)(2,1)S(1)}, bf16[128,3584]{1,0:T(8,128)(2,1)}, u32[]{:S(2)}) copy-start(bf16[128,3584]{1,0:T(8,128)(2,1)} %copy-done.4) | copy-start | bytes 2752516
  85.9 8.1 %copy-start.30 = (bf16[256,64]{1,0:T(8,128)(2,1)}, bf16[256,64]{1,0:T(8,128)(2,1)S(1)}, u32[]{:S(2)}) copy-start(bf16[256,64]{1,0:T(8,128)(2,1)S(1)} %get-tuple-element.87) | copy-start | bytes 98308
  87.9 7.4 %copy-start.1 = (bf16[256,2048]{1,0:T(8,128)(2,1)S(1)}, bf16[256,2048]{1,0:T(8,128)(2,1)}, u32[]{:S(2)}) copy-start(bf16[256,2048]{1,0:T(8,128)(2,1)} %all-gather.3.cloned.1.call-done) | copy-start | bytes 3145732
  99.3 4.2 copy-start.8
  107.6 126.1 %all-reduce.13.cloned.1.call-start = ((), (), s32[]{:S(2)}) async-start(), calls=%async_computation.6 | async-start | bytes 2752512 | tf_op jit(solution)/shard_map/psum | solution.py:224
  142.8 21.2 %copy-start = (bf16[4,64,384]{2,1,0:T(8,128)(2,1)S(1)}, bf16[4,64,384]{2,1,0:T(8,128)(2,1)}, u32[]{:S(2)}) copy-start(bf16[4,64,384]{2,1,0:T(8,128)(2,1)} %total_row.1) | copy-start | bytes 589828
  142.8 22.7 %copy-start.3 = (bf16[3584,64]{0,1:T(8,128)(2,1)S(1)}, bf16[3584,64]{0,1:T(8,128)(2,1)}, u32[]{:S(2)}) copy-start(bf16[3584,64]{0,1:T(8,128)(2,1)} %param.28) | copy-start | bytes 1376260
  142.8 24.0 %copy-start.6 = (bf16[64,3584]{1,0:T(8,128)(2,1)S(1)}, bf16[64,3584]{1,0:T(8,128)(2,1)}, u32[]{:S(2)}) copy-start(bf16[64,3584]{1,0:T(8,128)(2,1)} %param.27) | copy-start | bytes 1376260
  164.0 4.2 copy-start.18
  164.0 4.2 copy-start.19
  164.0 4.2 copy-start.45
  164.0 4.2 copy-start.47
  170.3 4.5 copy-start.61
  170.3 4.5 copy-start.63
  170.3 4.5 copy-start.65
  170.3 4.5 copy-start.67
  175.9 125.9 %all-reduce.11.cloned.1.call-start = ((), (), s32[]{:S(2)}) async-start(), calls=%async_computation.5 | async-start | bytes 2752512 | tf_op jit(solution)/shard_map/psum | solution.py:224
  176.0 6.4 %copy-start.66 = (bf16[256,896]{1,0:T(8,128)(2,1)S(1)}, bf16[256,896]{1,0:T(8,128)(2,1)}, u32[]{:S(2)}) copy-start(bf16[256,896]{1,0:T(8,128)(2,1)} %copy-done.65) | copy-start | bytes 1376260
  176.0 6.4 %copy-start.68 = (bf16[256,896]{1,0:T(8,128)(2,1)S(1)}, bf16[256,896]{1,0:T(8,128)(2,1)}, u32[]{:S(2)}) copy-start(bf16[256,896]{1,0:T(8,128)(2,1)} %copy-done.67) | copy-start | bytes 1376260
  182.4 6.5 %copy-start.62 = (bf16[256,896]{1,0:T(8,128)(2,1)S(1)}, bf16[256,896]{1,0:T(8,128)(2,1)}, u32[]{:S(2)}) copy-start(bf16[256,896]{1,0:T(8,128)(2,1)} %copy-done.61) | copy-start | bytes 1376260
  182.4 6.5 %copy-start.64 = (bf16[256,896]{1,0:T(8,128)(2,1)S(1)}, bf16[256,896]{1,0:T(8,128)(2,1)}, u32[]{:S(2)}) copy-start(bf16[256,896]{1,0:T(8,128)(2,1)} %copy-done.63) | copy-start | bytes 1376260
  237.8 4.3 copy-start.31
  237.8 5.3 %copy-start.34 = (f32[256,64]{0,1:T(8,128)S(1)}, f32[256,64]{0,1:T(8,128)}, u32[]{:S(2)}) copy-start(f32[256,64]{0,1:T(8,128)} %convolution_add_fusion.12) | copy-start | bytes 196612
  244.0 126.1 %all-reduce.9.cloned.1.call-start = ((), (), s32[]{:S(2)}) async-start(), calls=%async_computation.4 | async-start | bytes 2752512 | tf_op jit(solution)/shard_map/psum | solution.py:224
  244.1 6.6 %copy-start.21 = (bf16[256,896]{1,0:T(8,128)(2,1)S(1)}, bf16[256,896]{1,0:T(8,128)(2,1)}, u32[]{:S(2)}) copy-start(bf16[256,896]{1,0:T(8,128)(2,1)} %get-tuple-element.63) | copy-start | bytes 1376260
  244.1 6.6 %copy-start.23 = (bf16[256,896]{1,0:T(8,128)(2,1)S(1)}, bf16[256,896]{1,0:T(8,128)(2,1)}, u32[]{:S(2)}) copy-start(bf16[256,896]{1,0:T(8,128)(2,1)} %get-tuple-element.69) | copy-start | bytes 1376260
  244.1 6.6 %copy-start.69 = (f32[512,128]{0,1:T(8,128)S(1)}, f32[512,128]{0,1:T(8,128)}, u32[]{:S(2)}) copy-start(f32[512,128]{0,1:T(8,128)} %fusion.152) | copy-start | bytes 786436
  244.1 8.7 %copy-start.57 = (bf16[256,896]{1,0:T(8,128)(2,1)S(1)}, bf16[256,896]{1,0:T(8,128)(2,1)}, u32[]{:S(2)}) copy-start(bf16[256,896]{1,0:T(8,128)(2,1)} %get-tuple-element.64) | copy-start | bytes 1376260
  244.1 8.7 %copy-start.58 = (bf16[256,896]{1,0:T(8,128)(2,1)S(1)}, bf16[256,896]{1,0:T(8,128)(2,1)}, u32[]{:S(2)}) copy-start(bf16[256,896]{1,0:T(8,128)(2,1)} %get-tuple-element.74) | copy-start | bytes 1376260
  244.2 8.6 %copy-start.70 = (f32[512,128]{0,1:T(8,128)S(1)}, f32[512,128]{0,1:T(8,128)}, u32[]{:S(2)}) copy-start(f32[512,128]{0,1:T(8,128)} %fusion.151) | copy-start | bytes 786436
  305.9 4.3 copy-start.35
  312.4 138.9 %reduce-scatter.2.cloned.1.call-start = ((), (), s32[]{:S(2)}) async-start(), calls=%async_computation.3 | async-start | bytes 2359296 | tf_op jit(solution)/shard_map/reduce_scatter | solution.py:285
  312.8 4.8 %copy-start.59 = (bf16[256,896]{1,0:T(8,128)(2,1)S(1)}, bf16[256,896]{1,0:T(8,128)(2,1)}, u32[]{:S(2)}) copy-start(bf16[256,896]{1,0:T(8,128)(2,1)} %get-tuple-element.60) | copy-start | bytes 1376260
  312.8 4.8 %copy-start.60 = (bf16[256,896]{1,0:T(8,128)(2,1)S(1)}, bf16[256,896]{1,0:T(8,128)(2,1)}, u32[]{:S(2)}) copy-start(bf16[256,896]{1,0:T(8,128)(2,1)} %get-tuple-element.70) | copy-start | bytes 1376260
  312.9 5.8 %copy-start.51 = (bf16[256,896]{1,0:T(8,128)(2,1)S(1)}, bf16[256,896]{1,0:T(8,128)(2,1)}, u32[]{:S(2)}) copy-start(bf16[256,896]{1,0:T(8,128)(2,1)} %get-tuple-element.61) | copy-start | bytes 1376260
  312.9 5.8 %copy-start.52 = (bf16[256,896]{1,0:T(8,128)(2,1)S(1)}, bf16[256,896]{1,0:T(8,128)(2,1)}, u32[]{:S(2)}) copy-start(bf16[256,896]{1,0:T(8,128)(2,1)} %get-tuple-element.73) | copy-start | bytes 1376260
  312.9 5.7 %copy-start.71 = (f32[512,128]{0,1:T(8,128)S(1)}, f32[512,128]{0,1:T(8,128)}, u32[]{:S(2)}) copy-start(f32[512,128]{0,1:T(8,128)} %convolution_add_fusion.2) | copy-start | bytes 786436
  370.1 4.1 copy-start.50
  377.5 7.1 %copy-start.53 = (bf16[256,896]{1,0:T(8,128)(2,1)}, bf16[256,896]{1,0:T(8,128)(2,1)S(1)}, u32[]{:S(2)}) copy-start(bf16[256,896]{1,0:T(8,128)(2,1)S(1)} %get-tuple-element.58) | copy-start | bytes 1376260
  377.5 7.1 %copy-start.54 = (bf16[256,896]{1,0:T(8,128)(2,1)}, bf16[256,896]{1,0:T(8,128)(2,1)S(1)}, u32[]{:S(2)}) copy-start(bf16[256,896]{1,0:T(8,128)(2,1)S(1)} %get-tuple-element.72) | copy-start | bytes 1376260
  377.5 7.1 %copy-start.55 = (bf16[256,896]{1,0:T(8,128)(2,1)}, bf16[256,896]{1,0:T(8,128)(2,1)S(1)}, u32[]{:S(2)}) copy-start(bf16[256,896]{1,0:T(8,128)(2,1)S(1)} %get-tuple-element.57) | copy-start | bytes 1376260
  377.5 7.1 %copy-start.56 = (bf16[256,896]{1,0:T(8,128)(2,1)}, bf16[256,896]{1,0:T(8,128)(2,1)S(1)}, u32[]{:S(2)}) copy-start(bf16[256,896]{1,0:T(8,128)(2,1)S(1)} %get-tuple-element.71) | copy-start | bytes 1376260
  384.6 6.7 %copy-start.2 = (f32[512,2048]{1,0:T(8,128)S(1)}, f32[512,2048]{1,0:T(8,128)}, u32[]{:S(2)}) copy-start(f32[512,2048]{1,0:T(8,128)} %fusion.24) | copy-start | bytes 12582916
  384.6 6.7 %copy-start.22 = (bf16[256,896]{1,0:T(8,128)(2,1)S(1)}, bf16[256,896]{1,0:T(8,128)(2,1)}, u32[]{:S(2)}) copy-start(bf16[256,896]{1,0:T(8,128)(2,1)} %get-tuple-element.63) | copy-start | bytes 1376260
  384.6 6.7 %copy-start.24 = (bf16[256,896]{1,0:T(8,128)(2,1)S(1)}, bf16[256,896]{1,0:T(8,128)(2,1)}, u32[]{:S(2)}) copy-start(bf16[256,896]{1,0:T(8,128)(2,1)} %get-tuple-element.69) | copy-start | bytes 1376260
  406.3 34.0 %copy-start.32 = (bf16[256,64]{1,0:T(8,128)(2,1)S(1)}, bf16[256,64]{1,0:T(8,128)(2,1)}, u32[]{:S(2)}) copy-start(bf16[256,64]{1,0:T(8,128)(2,1)} %copy-done.30) | copy-start | bytes 98308
  414.1 30.8 %copy-start.9 = (bf16[256,2048]{1,0:T(8,128)(2,1)S(1)}, bf16[256,2048]{1,0:T(8,128)(2,1)}, u32[]{:S(2)}) copy-start(bf16[256,2048]{1,0:T(8,128)(2,1)} %all-gather.5.cloned.1.call-done) | copy-start | bytes 3145732
  439.5 5.3 %copy-start.20 = (bf16[8,32,320]{2,1,0:T(8,128)(2,1)S(1)}, bf16[8,32,320]{2,1,0:T(8,128)(2,1)}, u32[]{:S(2)}) copy-start(bf16[8,32,320]{2,1,0:T(8,128)(2,1)} %total_col.1) | copy-start | bytes 491524
  441.8 6.6 %copy-start.38 = (f32[896,64]{0,1:T(8,128)S(1)}, f32[896,64]{0,1:T(8,128)}, u32[]{:S(2)}) copy-start(f32[896,64]{0,1:T(8,128)} %convolution_multiply_fusion.32) | copy-start | bytes 688132
  441.8 6.6 %copy-start.39 = (f32[896,64]{0,1:T(8,128)S(1)}, f32[896,64]{0,1:T(8,128)}, u32[]{:S(2)}) copy-start(f32[896,64]{0,1:T(8,128)} %convolution_multiply_fusion.31) | copy-start | bytes 688132
  441.8 6.5 %copy-start.43 = (f32[896,64]{0,1:T(8,128)S(1)}, f32[896,64]{0,1:T(8,128)}, u32[]{:S(2)}) copy-start(f32[896,64]{0,1:T(8,128)} %convolution_multiply_fusion.30) | copy-start | bytes 688132
  444.8 4.5 copy-start.36
  444.9 4.5 copy-start.41
  444.9 4.5 copy-start.42
  446.0 4.3 copy-start.37
  446.0 4.3 copy-start.40
  446.0 4.3 copy-start.44
  447.2 5.1 %copy-start.10 = (bf16[2048,64]{0,1:T(8,128)(2,1)S(1)}, bf16[2048,64]{0,1:T(8,128)(2,1)}, u32[]{:S(2)}) copy-start(bf16[2048,64]{0,1:T(8,128)(2,1)} %param.24) | copy-start | bytes 786436
  447.2 5.1 %copy-start.11 = (bf16[2048,64]{0,1:T(8,128)(2,1)S(1)}, bf16[2048,64]{0,1:T(8,128)(2,1)}, u32[]{:S(2)}) copy-start(bf16[2048,64]{0,1:T(8,128)(2,1)} %param.26) | copy-start | bytes 786436
  (15 other events, 44.3 us)
Sparse Core Ops, SparseCore 0:
  21.5 21.6 all-gather.2
  44.8 21.8 all-gather.4
  107.7 56.2 all-reduce.14
  176.0 57.5 all-reduce.12
  244.2 57.5 all-reduce.10
  312.5 57.5 all-reduce.8
  403.9 39.6 reduce-scatter.1

commit v2 on v1

--- a/solution.py
+++ b/solution.py
@@ -158,6 +158,297 @@
     )
 
 
+def block_kernel(
+    x_ref,
+    cot_ref,
+    gate_hbm,
+    up_hbm,
+    down_hbm,
+    gate_left,
+    up_left,
+    adj_left,
+    gate_stack,
+    up_stack,
+    adj_stack,
+    gate_out,
+    up_out,
+    down_in,
+    feature_ref,
+    gate_q,
+    up_q,
+    low_q,
+    gate_curve,
+    up_curve,
+    down_curve,
+    parts,
+    first_in,
+    second_out,
+    second_in,
+    whole,
+    wide_buf,
+    down_buf,
+    total,
+    send_sem,
+    recv_sem,
+    wide_sem,
+    down_sem,
+):
+    me = lax.axis_index("row")
+    flip_low = me + 1 - 2 * lax.rem(me, 2)
+    flip_high = me + 2 - 4 * (me // 2)
+    flip_both = 3 - me
+    chunks, blocks, block, triple = parts.shape
+    width = triple // 3
+    count = x_ref.shape[0]
+    depth = x_ref.shape[1]
+    slots = wide_buf.shape[0]
+
+    barrier = pltpu.get_barrier_semaphore()
+    for peer in (flip_low, flip_high):
+        pl.semaphore_signal(barrier, inc=1, device_id={"row": peer}, device_id_type=MESH)
+
+    def lanes(c):
+        return pl.ds(pl.multiple_of(c * width, width), width)
+
+    def loads(c):
+        slot, side = lax.rem(c, slots), lax.rem(c, 2)
+        return [
+            pltpu.make_async_copy(
+                gate_hbm.at[:, lanes(c)], wide_buf.at[slot, 0], wide_sem.at[slot, 0]
+            ),
+            pltpu.make_async_copy(
+                up_hbm.at[:, lanes(c)], wide_buf.at[slot, 1], wide_sem.at[slot, 1]
+            ),
+            pltpu.make_async_copy(down_hbm.at[lanes(c), :], down_buf.at[side], down_sem.at[side]),
+        ]
+
+    def send(src, dst, c, path, k, peer):
+        return pltpu.make_async_remote_copy(
+            src_ref=src,
+            dst_ref=dst,
+            send_sem=send_sem.at[c, path, k],
+            recv_sem=recv_sem.at[c, path, k],
+            device_id={"row": peer},
+            device_id_type=MESH,
+        )
+
+    def ends(path):
+        return (flip_low, flip_high) if path == 0 else (flip_high, flip_low)
+
+    def sends(c, path, ks):
+        near, far = ends(path)
+        base = 4 * path
+        table = [
+            lambda: send(parts.at[c, base + near], first_in.at[c, path, 0], c, path, 0, near),
+            lambda: send(parts.at[c, base + flip_both], first_in.at[c, path, 1], c, path, 1, near),
+            lambda: send(second_out.at[c, path], second_in.at[c, path], c, path, 2, far),
+            lambda: send(whole.at[c, base + me], whole.at[c, base + me], c, path, 3, far),
+            lambda: send(whole.at[c, base + me], whole.at[c, base + me], c, path, 4, near),
+            lambda: send(whole.at[c, base + far], whole.at[c, base + far], c, path, 5, near),
+        ]
+        return [table[k]() for k in ks]
+
+    def arrivals(c, path, ks):
+        near, far = ends(path)
+        base = 4 * path
+        table = [
+            lambda: send(parts.at[c, base + me], first_in.at[c, path, 0], c, path, 0, near),
+            lambda: send(parts.at[c, base + far], first_in.at[c, path, 1], c, path, 1, near),
+            lambda: send(second_out.at[c, path], second_in.at[c, path], c, path, 2, far),
+            lambda: send(whole.at[c, base + far], whole.at[c, base + far], c, path, 3, far),
+            lambda: send(whole.at[c, base + near], whole.at[c, base + near], c, path, 4, near),
+            lambda: send(whole.at[c, base + flip_both], whole.at[c, base + flip_both], c, path, 5, near),
+        ]
+        return [table[k]() for k in ks]
+
+    def put(c, at, value):
+        parts[c, :, :, at * width : (at + 1) * width] = value.astype(jnp.bfloat16).reshape(
+            blocks, block, width
+        )
+
+    for copy in loads(0):
+        copy.start()
+    total[...] = jnp.zeros_like(total)
+    gate_q[...] = jnp.zeros_like(gate_q)
+    up_q[...] = jnp.zeros_like(up_q)
+    low_q[...] = jnp.zeros_like(low_q)
+    pl.semaphore_wait(barrier, 2)
+
+    def project(c):
+        for copy in loads(c):
+            copy.wait()
+
+        @pl.when(c + 1 < chunks)
+        def _():
+            for copy in loads(c + 1):
+                copy.start()
+
+        slot = lax.rem(c, slots)
+        put(c, 0, curvature_product(x_ref[...], wide_buf[slot, 0]))
+        put(c, 1, curvature_product(x_ref[...], wide_buf[slot, 1]))
+        put(c, 2, cross_shard_total(cot_ref[...], down_buf[lax.rem(c, 2)]))
+        for path in range(2):
+            for copy in sends(c, path, (0, 1)):
+                copy.start()
+
+    def relay(c):
+        for path in range(2):
+            near, far = ends(path)
+            for copy in arrivals(c, path, (0, 1)):
+                copy.wait_recv()
+            second_out[c, path] = (
+                parts[c, 4 * path + far].astype(jnp.float32)
+                + first_in[c, path, 1].astype(jnp.float32)
+            ).astype(jnp.bfloat16)
+            sends(c, path, (2,))[0].start()
+
+    def settle(c):
+        for path in range(2):
+            arrivals(c, path, (2,))[0].wait_recv()
+            whole[c, 4 * path + me] = (
+                parts[c, 4 * path + me].astype(jnp.float32)
+                + first_in[c, path, 0].astype(jnp.float32)
+                + second_in[c, path].astype(jnp.float32)
+            ).astype(jnp.bfloat16)
+            for copy in sends(c, path, (3, 4)):
+                copy.start()
+
+    def forward(c):
+        for path in range(2):
+            arrivals(c, path, (3,))[0].wait_recv()
+            sends(c, path, (5,))[0].start()
+
+    def differentiate(c):
+        for path in range(2):
+            for copy in arrivals(c, path, (4, 5)):
+                copy.wait_recv()
+
+        def got(at):
+            return (
+                whole[c, :, :, at * width : (at + 1) * width]
+                .reshape(count, width)
+                .astype(jnp.float32)
+            )
+
+        gate_w, up_w, down_w = gate_out[:, lanes(c)], up_out[:, lanes(c)], down_in[lanes(c), :]
+        gate_low = curvature_product(gate_left[...], gate_w)
+        up_low = curvature_product(up_left[...], up_w)
+        adj_low = cross_shard_total(adj_left[...], down_w)
+        hidden, hidden_dir, d_gate, d_up, d_gate_dir, d_up_dir = second_order(
+            got(0) + gate_low[:count],
+            got(1) + up_low[:count],
+            got(2) + adj_low[:count],
+            gate_low[count:],
+            up_low[count:],
+            adj_low[count:],
+        )
+        gate_d = jnp.concatenate([d_gate, d_gate_dir], axis=0)
+        up_d = jnp.concatenate([d_up, d_up_dir], axis=0)
+        hidden_d = jnp.concatenate([hidden_dir, hidden], axis=0)
+        gate_curve[:, lanes(c)] = curvature_product(gate_stack[...], gate_d)
+        up_curve[:, lanes(c)] = curvature_product(up_stack[...], up_d)
+        down_curve[:, lanes(c)] = curvature_product(adj_stack[...], hidden_d)
+        gate_q[...] += cross_shard_total(gate_d, gate_w)
+        up_q[...] += cross_shard_total(up_d, up_w)
+        low_q[...] += curvature_product(hidden_d, down_w)
+        slot = lax.rem(c, slots)
+        piece = 512 if depth % 512 == 0 else depth
+        for start in range(0, depth, piece):
+            span = slice(start, start + piece)
+            total[:, span] += cross_shard_total(
+                gate_d, wide_buf[slot, 0, span, :]
+            ) + cross_shard_total(up_d, wide_buf[slot, 1, span, :])
+
+    @pl.loop(0, chunks + 4)
+    def _(t):
+        for lag, stage in enumerate((project, relay, settle, forward, differentiate)):
+
+            @pl.when((t >= lag) & (t < chunks + lag))
+            def _(lag=lag, stage=stage):
+                stage(t - lag)
+
+    @pl.loop(0, chunks)
+    def _(c):
+        for path in range(2):
+            for copy in sends(c, path, range(6)):
+                copy.wait_send()
+
+    feature_ref[...] = total[...].astype(jnp.bfloat16)
+
+
+def fused_block(x, cot, gate_w, up_w, down_w, ranks, gate_out, up_out, down_in, width):
+    count, depth = x.shape
+    columns = gate_w.shape[1]
+    rank = ranks.shape[1] // 6
+    chunks = columns // width
+    half = ranks * adapter_scale
+    gate, up, gate_dir, up_dir, adj, adj_dir = [
+        half[:, index * rank : (index + 1) * rank] for index in range(6)
+    ]
+    empty = jnp.zeros_like(gate)
+
+    def left(low, low_dir):
+        return jnp.concatenate(
+            [
+                jnp.concatenate([low, empty], axis=1),
+                jnp.concatenate([low_dir, low], axis=1),
+            ],
+            axis=0,
+        )
+
+    vmem = pl.BlockSpec(memory_space=pltpu.VMEM)
+    anywhere = pl.BlockSpec(memory_space=pl.ANY)
+    block = count // 8
+    f32, bf16 = jnp.float32, jnp.bfloat16
+    return pl.pallas_call(
+        block_kernel,
+        out_shape=[
+            jax.ShapeDtypeStruct((2 * count, depth), bf16),
+            jax.ShapeDtypeStruct((2 * count, 2 * rank), f32),
+            jax.ShapeDtypeStruct((2 * count, 2 * rank), f32),
+            jax.ShapeDtypeStruct((2 * count, 2 * rank), f32),
+            jax.ShapeDtypeStruct((rank, columns), f32),
+            jax.ShapeDtypeStruct((rank, columns), f32),
+            jax.ShapeDtypeStruct((rank, columns), f32),
+        ],
+        in_specs=[vmem] * 2 + [anywhere] * 3 + [vmem] * 9,
+        out_specs=[vmem] * 7,
+        scratch_shapes=[
+            pltpu.VMEM((chunks, 8, block, 3 * width), bf16),
+            pltpu.VMEM((chunks, 2, 2, block, 3 * width), bf16),
+            pltpu.VMEM((chunks, 2, block, 3 * width), bf16),
+            pltpu.VMEM((chunks, 2, block, 3 * width), bf16),
+            pltpu.VMEM((chunks, 8, block, 3 * width), bf16),
+            pltpu.VMEM((6, 2, depth, width), bf16),
+            pltpu.VMEM((2, width, depth), bf16),
+            pltpu.VMEM((2 * count, depth), f32),
+            pltpu.SemaphoreType.DMA((chunks, 2, 6)),
+            pltpu.SemaphoreType.DMA((chunks, 2, 6)),
+            pltpu.SemaphoreType.DMA((6, 2)),
+            pltpu.SemaphoreType.DMA((2,)),
+        ],
+        compiler_params=pltpu.CompilerParams(
+            collective_id=2, has_side_effects=True, vmem_limit_bytes=60 * 1024 * 1024
+        ),
+        name="block",
+    )(
+        x,
+        cot,
+        gate_w,
+        up_w,
+        down_w,
+        left(gate, gate_dir),
+        left(up, up_dir),
+        left(adj, adj_dir),
+        jnp.concatenate([gate_dir, gate], axis=0).T,
+        jnp.concatenate([up_dir, up], axis=0).T,
+        jnp.concatenate([adj, adj_dir], axis=0).T,
+        gate_out,
+        up_out,
+        down_in,
+    )
+
+
 def chunk_count(width):
     for count in (4, 2):
         if width % (128 * count) == 0:
@@ -197,10 +488,6 @@
     )
     normed_tokens = lax.all_gather(own_normed, "col", axis=0, tiled=True)
     count = normed_tokens.shape[0]
-    chunks = chunk_count(width_columns)
-    wide = width_columns // chunks
-    spans = [slice(index * wide, (index + 1) * wide) for index in range(chunks)]
-
     in_factors = jnp.concatenate(
         [
             gate_input_factor,
@@ -212,75 +499,99 @@
     )
     out_factors = jnp.concatenate([down_b, down_b_dir], axis=0)
 
-    summed_chunks = []
-    for span in spans:
-        partial = (
-            curvature_product(normed_tokens, gate_frozen_weight[:, span]).astype(jnp.bfloat16),
-            curvature_product(normed_tokens, up_frozen_weight[:, span]).astype(jnp.bfloat16),
-            cross_shard_total(cot_panel, down_frozen_weight[span]).astype(jnp.bfloat16),
-        )
-        if summed_chunks:
-            partial, summed_chunks[-1] = lax.optimization_barrier((partial, summed_chunks[-1]))
-        summed_chunks.append(lax.psum(partial, "row"))
-
     projected = jnp.concatenate(
         [curvature_product(normed_tokens, in_factors), cross_shard_total(cot_panel, out_factors)],
         axis=1,
     )
     ranks = shard_total(projected, "row", 0)
-    gate_low, up_low, gate_low_dir, up_low_dir, adj_low, adj_low_dir = [
-        ranks[:, index * rank : (index + 1) * rank] for index in range(6)
-    ]
-    gate_pair = jnp.concatenate([gate_low_dir, gate_low], axis=1)
-    up_pair = jnp.concatenate([up_low_dir, up_low], axis=1)
-    adj_pair = jnp.concatenate([adj_low_dir, adj_low], axis=1)
-    gate_stack = jnp.concatenate([gate_low_dir, gate_low], axis=0)
-    up_stack = jnp.concatenate([up_low_dir, up_low], axis=0)
-    adj_stack = jnp.concatenate([adj_low, adj_low_dir], axis=0)
     gate_out = jnp.concatenate([gate_output_factor, gate_output_factor_direction], axis=0)
     up_out = jnp.concatenate([up_output_factor, up_output_factor_direction], axis=0)
     down_in = jnp.concatenate([down_input_factor, down_input_factor_direction], axis=1)
 
-    feature = 0.0
-    gate_q = 0.0
-    up_q = 0.0
-    low_dir = 0.0
-    gate_output, up_output, down_input = [], [], []
-    for span, total in zip(spans, summed_chunks):
-        gate_sum, up_sum, adj_sum = [value.astype(jnp.float32) for value in total]
-        gate_pre = gate_sum + adapter_scale * curvature_product(
-            gate_low, gate_output_factor[:, span]
-        )
-        up_pre = up_sum + adapter_scale * curvature_product(
-            up_low, up_output_factor[:, span]
-        )
-        hidden_adj = adj_sum + adapter_scale * cross_shard_total(
-            adj_low, down_input_factor[span]
-        )
-        gate_tan = adapter_scale * curvature_product(gate_pair, gate_out[:, span])
-        up_tan = adapter_scale * curvature_product(up_pair, up_out[:, span])
-        adj_tan = adapter_scale * cross_shard_total(adj_pair, down_in[span])
-        hidden, hidden_dir, d_gate, d_up, d_gate_dir, d_up_dir = second_order(
-            gate_pre, up_pre, hidden_adj, gate_tan, up_tan, adj_tan
-        )
-        gate_d = jnp.concatenate([d_gate, d_gate_dir], axis=0)
-        up_d = jnp.concatenate([d_up, d_up_dir], axis=0)
-        hidden_d = jnp.concatenate([hidden_dir, hidden], axis=0)
-        gate_output.append(adapter_scale * summed_over_rows(gate_stack, gate_d))
-        up_output.append(adapter_scale * summed_over_rows(up_stack, up_d))
-        down_input.append(adapter_scale * summed_over_rows(hidden_d, adj_stack))
-        gate_q = gate_q + cross_shard_total(gate_d, gate_out[:, span])
-        up_q = up_q + cross_shard_total(up_d, up_out[:, span])
-        low_dir = (
-            low_dir
-            + curvature_product(hidden_dir, down_input_factor[span])
-            + curvature_product(hidden, down_input_factor_direction[span])
-        )
-        feature = (
-            feature
-            + cross_shard_total(gate_d, gate_frozen_weight[:, span])
-            + cross_shard_total(up_d, up_frozen_weight[:, span])
-        )
+    width = 256
+    if lax.axis_size("row") == 4 and width_columns % width == 0 and count % 128 == 0:
+        feature, gate_q, up_q, low_q, gate_output, up_output, down_input = fused_block(
+            normed_tokens,
+            cot_panel,
+            gate_frozen_weight,
+            up_frozen_weight,
+            down_frozen_weight,
+            ranks,
+            gate_out,
+            up_out,
+            down_in,
+            width,
+        )
+        low_dir = low_q[:count, :rank] + low_q[count:, rank:]
+        down_input = down_input.T
+    else:
+        chunks = chunk_count(width_columns)
+        wide = width_columns // chunks
+        spans = [slice(index * wide, (index + 1) * wide) for index in range(chunks)]
+
+        summed_chunks = []
+        for span in spans:
+            partial = (
+                curvature_product(normed_tokens, gate_frozen_weight[:, span]).astype(jnp.bfloat16),
+                curvature_product(normed_tokens, up_frozen_weight[:, span]).astype(jnp.bfloat16),
+                cross_shard_total(cot_panel, down_frozen_weight[span]).astype(jnp.bfloat16),
+            )
+            if summed_chunks:
+                partial, summed_chunks[-1] = lax.optimization_barrier((partial, summed_chunks[-1]))
+            summed_chunks.append(lax.psum(partial, "row"))
+
+        gate_low, up_low, gate_low_dir, up_low_dir, adj_low, adj_low_dir = [
+            ranks[:, index * rank : (index + 1) * rank] for index in range(6)
+        ]
+        gate_pair = jnp.concatenate([gate_low_dir, gate_low], axis=1)
+        up_pair = jnp.concatenate([up_low_dir, up_low], axis=1)
+        adj_pair = jnp.concatenate([adj_low_dir, adj_low], axis=1)
+        gate_stack = jnp.concatenate([gate_low_dir, gate_low], axis=0)
+        up_stack = jnp.concatenate([up_low_dir, up_low], axis=0)
+        adj_stack = jnp.concatenate([adj_low, adj_low_dir], axis=0)
+        feature = 0.0
+        gate_q = 0.0
+        up_q = 0.0
+        low_dir = 0.0
+        gate_output, up_output, down_input = [], [], []
+        for span, total in zip(spans, summed_chunks):
+            gate_sum, up_sum, adj_sum = [value.astype(jnp.float32) for value in total]
+            gate_pre = gate_sum + adapter_scale * curvature_product(
+                gate_low, gate_output_factor[:, span]
+            )
+            up_pre = up_sum + adapter_scale * curvature_product(
+                up_low, up_output_factor[:, span]
+            )
+            hidden_adj = adj_sum + adapter_scale * cross_shard_total(
+                adj_low, down_input_factor[span]
+            )
+            gate_tan = adapter_scale * curvature_product(gate_pair, gate_out[:, span])
+            up_tan = adapter_scale * curvature_product(up_pair, up_out[:, span])
+            adj_tan = adapter_scale * cross_shard_total(adj_pair, down_in[span])
+            hidden, hidden_dir, d_gate, d_up, d_gate_dir, d_up_dir = second_order(
+                gate_pre, up_pre, hidden_adj, gate_tan, up_tan, adj_tan
+            )
+            gate_d = jnp.concatenate([d_gate, d_gate_dir], axis=0)
+            up_d = jnp.concatenate([d_up, d_up_dir], axis=0)
+            hidden_d = jnp.concatenate([hidden_dir, hidden], axis=0)
+            gate_output.append(adapter_scale * summed_over_rows(gate_stack, gate_d))
+            up_output.append(adapter_scale * summed_over_rows(up_stack, up_d))
+            down_input.append(adapter_scale * summed_over_rows(hidden_d, adj_stack))
+            gate_q = gate_q + cross_shard_total(gate_d, gate_out[:, span])
+            up_q = up_q + cross_shard_total(up_d, up_out[:, span])
+            low_dir = (
+                low_dir
+                + curvature_product(hidden_dir, down_input_factor[span])
+                + curvature_product(hidden, down_input_factor_direction[span])
+            )
+            feature = (
+                feature
+                + cross_shard_total(gate_d, gate_frozen_weight[:, span])
+                + cross_shard_total(up_d, up_frozen_weight[:, span])
+            )
+        gate_output = jnp.concatenate(gate_output, axis=1)
+        up_output = jnp.concatenate(up_output, axis=1)
+        down_input = jnp.concatenate(down_input, axis=0)
 
     summed = lax.psum_scatter(
         feature.astype(jnp.bfloat16).reshape(2, count, width_rows),
@@ -318,10 +629,10 @@
         normed_feature_adjoint,
         normed_feature_adjoint_direction,
         gate_input,
-        jnp.concatenate(gate_output, axis=1),
+        gate_output,
         up_input,
-        jnp.concatenate(up_output, axis=1),
-        jnp.concatenate(down_input, axis=0),
+        up_output,
+        down_input,
         down_output,
     )
 

time: 470 us -> 247 us (0.53); the launches traced: 461 us -> 247 us
  matrix products: 203 us -> 11.4 us
  waiting for transfers between devices: 164 us -> 47.5 us
  Pallas kernels: 32.9 us -> 138 us
  local copies, waits for them, and re-layouts: 24.1 us -> 14.3 us
    psum x4 -> x0, waiting for transfers between devices: 132 us -> none  [on_device(): summed_chunks.append(lax.psum(partial, 'row'))]
    pallas_call x0 -> x1, Pallas kernels: none -> 106 us  [fused_block(): pl.pallas_call(block_kernel, out_shape=[jax.ShapeDtypeStruct((2 * count,...]
    dot_general x31 -> x3, matrix products: 105 us -> 3.62 us  [cross_shard_total(): lax.dot_general(left, right, (((1,), (1,)), ((), ())), preferred_element_...]
    dot_general x33 -> x1, matrix products: 74.3 us -> 1.7 us  [curvature_product(): return jnp.dot(left, right, preferred_element_type=jnp.float32)]
    dot_general x15 -> x3, matrix products: 24.4 us -> 6.05 us  [summed_over_rows(): lax.dot_general(left, right, (((0,), (0,)), ((), ())), preferred_element_...]
    reduce_scatter x1, waiting for transfers between devices: 0.01 us -> 12.5 us  [on_device(): lax.psum_scatter(feature.astype(jnp.bfloat16).reshape(2, count, width_row...]
    unnamed x150 -> x53, local copies, waits for them, and re-layouts: 9.41 us -> 8.39 us
  transfers between devices with their start and end apart: 7 -> 3, of which waited for: 6 -> 3; matrix products, arithmetic and copies ran while one was open for 30% -> 7% of each run, Pallas kernels for 4% -> 7%
where the time goes in v2:
time: 247 us
  Pallas kernels  138 us (56%)
  waiting for transfers between devices  47.5 us (19%)
  local copies, waits for them, and re-layouts  14.3 us (6%)
  between operations  14.1 us (6%)
  blocking collectives  11.4 us (5%)
  matrix products  11.4 us (5%)
  other arithmetic  10.3 us (4%)
    pallas_call x1, Pallas kernels, fused_block(): pl.pallas_call(block_kernel, out_shape=[jax.ShapeDtypeStruct((2 * count,...  106 us
    pallas_call x2, Pallas kernels, shard_total(): pl.pallas_call(functools.partial(total_kernel, axis, n), out_shape=jax.Sh...  31.8 us
    all_gather x1, waiting for transfers between devices, on_device(): cot_panel = lax.all_gather(cotangent, 'col', axis=0, tiled=True)  21.8 us
    reduce_scatter x1, waiting for transfers between devices, on_device(): lax.psum_scatter(feature.astype(jnp.bfloat16).reshape(2, count, width_row...  12.5 us
    all_gather x1, waiting for transfers between devices, on_device(): normed_tokens = lax.all_gather(own_normed, 'col', axis=0, tiled=True)  12.5 us
    psum x1, blocking collectives, on_device(): squares = lax.psum(jnp.sum(tokens_f * tokens_f, axis=1), 'row')  11.4 us
    unnamed x53, local copies, waits for them, and re-layouts  8.39 us
    dot_general x3, matrix products, summed_over_rows(): lax.dot_general(left, right, (((0,), (0,)), ((), ())), preferred_element_...  6.05 us
  transfers between devices with their start and end apart: 3, of which 3 were waited for; matrix products, arithmetic and copies ran while one was open for 7% of the time, Pallas kernels for 7%

profile of v2, /device:TPU:0, one launch (start us, length us, event | category | flops | bytes accessed | tf_op | source)
XLA Modules:
  0.0 246.7 jit_solution(3040969633349998969)
XLA Ops:
  7.2 0.0 all-gather.3.cloned.1.call-start
  7.2 1.0 fusion.8
  8.2 11.4 %psum.7 = f32[32]{0:T(128)S(1)} all-reduce(f32[32]{0:T(128)S(1)} %fusion.8), channel_id=1, replica_groups=mesh['row'=4,'col'=8] {'row'}, use_global_device_ids=true, to_apply=%region_1.0 | all-reduce | flops 32 | bytes 256 | tf_op jit(solution)/shard_map/psum | solution.py:485
  19.6 1.7 fusion.10
  21.3 0.0 all-gather.3.cloned.1.call-update
  21.3 0.0 all-gather.5.cloned.1.call-start
  21.4 0.7 all-gather.5.cloned.1.call-update
  22.1 0.0 copy-start.14
  22.1 0.0 reduce-scatter.2.cloned.1.call-start
  22.1 1.0 constant_dynamic-update-slice_fusion.3
  23.2 1.4 copy.41
  24.6 1.5 copy.42
  26.1 0.0 copy-start.8
  26.1 0.0 copy-start.9
  26.2 1.0 constant_dynamic-update-slice_fusion
  27.2 0.0 copy-start.10
  27.2 0.0 copy-start.11
  27.2 1.4 pad_maximum_fusion.2.down_in
  28.7 1.0 pad_maximum_fusion.gate_out
  29.7 1.0 pad_maximum_fusion.1.up_out
  30.6 12.5 %all-gather.3.cloned.1.call-done.x_ref = bf16[256,2048]{1,0:T(8,128)(2,1)} async-done(((bf16[32,2048]{1,0:T(8,128)(2,1)}), bf16[256,2048]{1,0:T(8,128)(2,1)}) %all-gather.3.cloned.1.call-update) | async-done | bytes 1048592 | tf_op jit(solution)/shard_map/all_gather | solution.py:489
  43.1 1.7 fusion.26
  44.8 21.8 %all-gather.5.cloned.1.call-done.cot_ref = bf16[256,2048]{1,0:T(8,128)(2,1)} async-done(((bf16[32,2048]{1,0:T(8,128)(2,1)}), bf16[256,2048]{1,0:T(8,128)(2,1)}) %all-gather.5.cloned.1.call-update) | async-done | bytes 1048592 | tf_op jit(solution)/shard_map/all_gather | solution.py:483
  66.6 0.0 copy-done.17
  66.6 1.7 convolution_bitcast_fusion
  68.3 0.9 copy.33
  69.2 14.3 %total_row.1 = bf16[4,64,384]{2,1,0:T(8,128)(2,1)} custom-call(f32[4,64,384]{2,1,0:T(8,128)} %bitcast.37), custom_call_target="tpu_custom_call" | custom-call | tf_op jit(solution)/shard_map/total_row/pallas_call | solution.py:91
  83.6 1.0 broadcast_multiply_fusion
  84.5 0.1 fusion.25
  84.7 0.1 copy.51
  84.8 0.1 copy.52
  84.9 0.6 maximum_bitcast_fusion.2.adj_stack
  85.5 0.1 copy.49
  85.6 0.1 copy.50
  85.7 0.6 maximum_bitcast_fusion.1.up_stack
  86.3 0.1 copy.47
  86.4 0.1 copy.48
  86.5 0.1 copy.46
  86.6 0.0 copy-done.16
  86.7 0.1 broadcast_select_fusion
  86.7 0.6 maximum_bitcast_fusion.gate_stack
  87.4 0.8 copy.43.gate_left
  88.2 0.8 copy.45.adj_left
  88.9 0.8 copy.44.up_left
  89.7 105.8 %block.1 = (bf16[512,2048]{1,0:T(8,128)(2,1)}, f32[512,128]{1,0:T(8,128)}, f32[512,128]{1,0:T(8,128)}, f32[512,128]{1,0:T(8,128)}, f32[64,3584]{1,0:T(8,128)}, /*index=5*/f32[64,3584]{1,0:T(8,128)}, f32[64,3584]{1,0:T(8,128)}) custom-call(bf16[256,2048]{1,0:T(8,128)(2,1)} %all-gather.3.cloned.1.call-done.x_ref, ...), custom_call_target="tpu_custom_call" | custom-call | tf_op jit(solution)/shard_map/block/pallas_call | solution.py:403
  195.6 0.0 reduce-scatter.2.cloned.1.call-update
  195.6 0.9 copy-done.13
  196.5 0.1 copy-done.12
  196.6 0.1 add_convert_fusion.2
  196.7 0.1 add_convert_fusion
  196.8 0.8 concatenate.98.x_ref
  197.6 17.5 %total_col.1 = bf16[8,32,320]{2,1,0:T(8,128)(2,1)} custom-call(bf16[8,32,320]{2,1,0:T(8,128)(2,1)} %concatenate.98.x_ref), custom_call_target="tpu_custom_call" | custom-call | tf_op jit(solution)/shard_map/total_col/pallas_call | solution.py:91
  215.2 0.7 fusion.24
  215.9 2.0 convolution_multiply_fusion.1
  218.0 2.0 convolution_multiply_fusion.2
  220.0 2.0 convolution_multiply_fusion
  222.0 12.5 %reduce-scatter.2.cloned.1.call-done = bf16[2,32,2048]{2,1,0:T(8,128)(2,1)} async-done(((bf16[2,256,2048]{2,1,0:T(8,128)(2,1)}), bf16[2,32,2048]{2,1,0:T(8,128)(2,1)}) %reduce-scatter.2.cloned.1.call-update) | async-done | bytes 262160 | tf_op jit(solution)/shard_map/reduce_scatter | solution.py:596
  234.5 1.0 convert_element_type.13
  235.5 0.9 fusion.1
  236.4 1.0 fusion
  237.4 0.9 copy.59
  238.4 0.9 copy.60
  239.3 0.0 copy-done.5
  239.3 0.9 copy.61
  (38 shorter events, 0.2 us)
Async XLA Ops:
  7.2 35.9 %all-gather.3.cloned.1.call-start = ((), (), s32[]{:S(2)}) async-start(), calls=%async_computation.1 | async-start | bytes 1179648 | tf_op jit(solution)/shard_map/all_gather | solution.py:489
  21.3 4.8 %copy-start.3 = (bf16[2048,64]{0,1:T(8,128)(2,1)S(1)}, bf16[2048,64]{0,1:T(8,128)(2,1)}, u32[]{:S(2)}) copy-start(bf16[2048,64]{0,1:T(8,128)(2,1)} %param.26) | copy-start | bytes 786436
  21.3 45.2 %all-gather.5.cloned.1.call-start = ((), (), s32[]{:S(2)}) async-start(), calls=%async_computation.2 | async-start | bytes 1179648 | tf_op jit(solution)/shard_map/all_gather | solution.py:483
  22.1 4.0 %copy-start.14 = (bf16[2048,64]{0,1:T(8,128)(2,1)S(1)}, bf16[2048,64]{0,1:T(8,128)(2,1)}, u32[]{:S(2)}) copy-start(bf16[2048,64]{0,1:T(8,128)(2,1)} %param.30) | copy-start | bytes 786436
  22.1 212.4 %reduce-scatter.2.cloned.1.call-start = ((), (), s32[]{:S(2)}) async-start(), calls=%async_computation.3 | async-start | bytes 2359296 | tf_op jit(solution)/shard_map/reduce_scatter | solution.py:596
  26.1 2.6 %copy-start.8 = (bf16[64,3584]{1,0:T(8,128)(2,1)S(1)}, bf16[64,3584]{1,0:T(8,128)(2,1)}, u32[]{:S(2)}) copy-start(bf16[64,3584]{1,0:T(8,128)(2,1)} %param.31) | copy-start | bytes 1376260
  26.1 2.5 %copy-start.9 = (bf16[64,3584]{1,0:T(8,128)(2,1)S(1)}, bf16[64,3584]{1,0:T(8,128)(2,1)}, u32[]{:S(2)}) copy-start(bf16[64,3584]{1,0:T(8,128)(2,1)} %param.25) | copy-start | bytes 1376260
  27.2 2.4 copy-start.10
  27.2 2.4 copy-start.11
  29.7 36.9 %copy-start.17 = (bf16[64,2048]{1,0:T(8,128)(2,1)S(1)}, bf16[64,2048]{1,0:T(8,128)(2,1)}, u32[]{:S(2)}) copy-start(bf16[64,2048]{1,0:T(8,128)(2,1)} %param.35) | copy-start | bytes 786436
  29.7 36.9 %copy-start.18 = (bf16[64,2048]{1,0:T(8,128)(2,1)S(1)}, bf16[64,2048]{1,0:T(8,128)(2,1)}, u32[]{:S(2)}) copy-start(bf16[64,2048]{1,0:T(8,128)(2,1)} %param.29) | copy-start | bytes 786436
  69.2 17.4 %copy-start.16 = (pred[128]{0:T(512)(128)(4,1)S(1)}, pred[128]{0:T(512)(128)(4,1)}, u32[]{:S(2)}) copy-start(pred[128]{0:T(512)(128)(4,1)} %constant.4.clone.1) | copy-start | bytes 388
  195.5 1.0 copy-start.13
  195.5 1.0 copy-start.12
  195.5 1.1 copy-start.15
  195.5 20.4 %copy-start = (bf16[256,2048]{1,0:T(8,128)(2,1)S(1)}, bf16[256,2048]{1,0:T(8,128)(2,1)}, u32[]{:S(2)}) copy-start(bf16[256,2048]{1,0:T(8,128)(2,1)} %all-gather.3.cloned.1.call-done.x_ref) | copy-start | bytes 3145732
  197.6 22.3 %copy-start.1 = (bf16[256,2048]{1,0:T(8,128)(2,1)S(1)}, bf16[256,2048]{1,0:T(8,128)(2,1)}, u32[]{:S(2)}) copy-start(bf16[256,2048]{1,0:T(8,128)(2,1)} %all-gather.5.cloned.1.call-done.cot_ref) | copy-start | bytes 3145732
  218.0 17.5 %copy-start.2 = (bf16[2048,64]{0,1:T(8,128)(2,1)S(1)}, bf16[2048,64]{0,1:T(8,128)(2,1)}, u32[]{:S(2)}) copy-start(bf16[2048,64]{0,1:T(8,128)(2,1)} %param.24) | copy-start | bytes 786436
  220.0 15.5 %copy-start.4 = (bf16[2048,64]{0,1:T(8,128)(2,1)S(1)}, bf16[2048,64]{0,1:T(8,128)(2,1)}, u32[]{:S(2)}) copy-start(bf16[2048,64]{0,1:T(8,128)(2,1)} %param.26) | copy-start | bytes 786436
  222.0 15.5 %copy-start.7 = (f32[64,3584]{1,0:T(8,128)S(1)}, f32[64,3584]{1,0:T(8,128)}, u32[]{:S(2)}) copy-start(f32[64,3584]{1,0:T(8,128)} %get-tuple-element.43) | copy-start | bytes 2752516
  236.4 1.9 copy-start.6
  237.4 1.9 copy-start.5
Sparse Core Ops, SparseCore 0:
  21.5 21.5 all-gather.2
  44.7 21.8 all-gather.4
  195.7 38.7 reduce-scatter.1

commit v3 on v2

--- a/solution.py
+++ b/solution.py
@@ -449,6 +449,166 @@
     )
 
 
+def gather_kernel(
+    tokens,
+    gain,
+    cot,
+    x_all,
+    cot_all,
+    x_buf,
+    cot_buf,
+    squares,
+    square_send,
+    square_recv,
+    far_send,
+    far_recv,
+    near_send,
+    near_recv,
+):
+    rows, columns = lax.axis_size("row"), lax.axis_size("col")
+    chips = columns // 2
+    my_row, me = lax.axis_index("row"), lax.axis_index("col")
+    partner = me + 1 - 2 * lax.rem(me, 2)
+    features = rows * tokens.shape[1]
+    barrier = pltpu.get_barrier_semaphore()
+
+    def row_peer(k):
+        return {"row": lax.rem(my_row + k, rows)}
+
+    def far_peer(k):
+        return {"col": lax.rem(me + 2 * k, columns)}
+
+    @pl.loop(1, rows)
+    def _(k):
+        pl.semaphore_signal(barrier, inc=1, device_id=row_peer(k), device_id_type=MESH)
+
+    @pl.loop(1, chips)
+    def _(k):
+        pl.semaphore_signal(barrier, inc=1, device_id=far_peer(k), device_id_type=MESH)
+
+    pl.semaphore_signal(barrier, inc=1, device_id={"col": partner}, device_id_type=MESH)
+
+    buffers = (cot_buf, x_buf)
+
+    def origin(k):
+        return lax.rem(me - 2 * k + columns, columns)
+
+    def square(k):
+        return pltpu.make_async_remote_copy(
+            src_ref=squares.at[0],
+            dst_ref=squares.at[k],
+            send_sem=square_send.at[k],
+            recv_sem=square_recv.at[k],
+            device_id=row_peer(k),
+            device_id_type=MESH,
+        )
+
+    def far(which, k, slot):
+        return pltpu.make_async_remote_copy(
+            src_ref=buffers[which].at[slot],
+            dst_ref=buffers[which].at[slot],
+            send_sem=far_send.at[which, k],
+            recv_sem=far_recv.at[which, k],
+            device_id=far_peer(k),
+            device_id_type=MESH,
+        )
+
+    def near(which, k, slot):
+        return pltpu.make_async_remote_copy(
+            src_ref=buffers[which].at[slot],
+            dst_ref=buffers[which].at[slot],
+            send_sem=near_send.at[which, k],
+            recv_sem=near_recv.at[which, k],
+            device_id={"col": partner},
+            device_id_type=MESH,
+        )
+
+    def launch(which):
+        @pl.loop(1, chips)
+        def _(k):
+            far(which, k, me).start()
+
+        near(which, 0, me).start()
+
+    values = tokens[...].astype(jnp.float32)
+    squares[0] = jnp.broadcast_to(
+        jnp.sum(values * values, axis=1, keepdims=True), squares.shape[1:]
+    )
+    cot_buf[me] = cot[...]
+    pl.semaphore_wait(barrier, rows + chips - 1)
+
+    @pl.loop(1, rows)
+    def _(k):
+        square(k).start()
+
+    launch(0)
+
+    def add(k, total):
+        square(k).wait_recv()
+        return total + squares[k]
+
+    total = lax.fori_loop(1, rows, add, squares[0])
+    scale = lax.rsqrt(total[:, :1] / features + epsilon)
+    x_buf[me] = (tokens[...].astype(jnp.float32) * scale * gain[...]).astype(jnp.bfloat16)
+    launch(1)
+    for which in range(2):
+
+        @pl.loop(1, chips)
+        def _(k, which=which):
+            far(which, k, origin(k)).wait_recv()
+            near(which, k, origin(k)).start()
+
+    for which in range(2):
+
+        @pl.loop(0, chips)
+        def _(k, which=which):
+            near(which, k, lax.rem(partner - 2 * k + columns, columns)).wait_recv()
+
+    @pl.loop(1, rows)
+    def _(k):
+        square(k).wait_send()
+
+    for which in range(2):
+
+        @pl.loop(1, chips)
+        def _(k, which=which):
+            far(which, k, me).wait_send()
+
+        @pl.loop(0, chips)
+        def _(k, which=which):
+            near(which, k, origin(k)).wait_send()
+
+    cot_all[...] = cot_buf[...]
+    x_all[...] = x_buf[...]
+
+
+def gathered(tokens, gain, cot):
+    rows, columns = lax.axis_size("row"), lax.axis_size("col")
+    own, depth = tokens.shape
+    whole = (columns, own, depth)
+    vmem = pl.BlockSpec(memory_space=pltpu.VMEM)
+    x, panel = pl.pallas_call(
+        gather_kernel,
+        out_shape=[jax.ShapeDtypeStruct(whole, jnp.bfloat16)] * 2,
+        in_specs=[vmem] * 3,
+        out_specs=[vmem] * 2,
+        scratch_shapes=[
+            pltpu.VMEM(whole, jnp.bfloat16),
+            pltpu.VMEM(whole, jnp.bfloat16),
+            pltpu.VMEM((rows, own, 128), jnp.float32),
+            pltpu.SemaphoreType.DMA((rows,)),
+            pltpu.SemaphoreType.DMA((rows,)),
+            pltpu.SemaphoreType.DMA((2, columns // 2)),
+            pltpu.SemaphoreType.DMA((2, columns // 2)),
+            pltpu.SemaphoreType.DMA((2, columns // 2)),
+            pltpu.SemaphoreType.DMA((2, columns // 2)),
+        ],
+        compiler_params=pltpu.CompilerParams(collective_id=3, has_side_effects=True),
+        name="gather",
+    )(tokens, gain.reshape(1, depth), cot)
+    return x.reshape(columns * own, depth), panel.reshape(columns * own, depth)
+
+
 def chunk_count(width):
     for count in (4, 2):
         if width % (128 * count) == 0:
@@ -478,15 +638,8 @@
 ):
     rank = gate_input_factor.shape[1]
     width_rows, width_columns = gate_frozen_weight.shape
-    features = width_rows * lax.axis_size("row")
     own_count = tokens.shape[0]
-    cot_panel = lax.all_gather(cotangent, "col", axis=0, tiled=True)
-    tokens_f = tokens.astype(jnp.float32)
-    squares = lax.psum(jnp.sum(tokens_f * tokens_f, axis=1), "row")
-    own_normed = (tokens_f * lax.rsqrt(squares[:, None] / features + epsilon) * norm_gain).astype(
-        jnp.bfloat16
-    )
-    normed_tokens = lax.all_gather(own_normed, "col", axis=0, tiled=True)
+    normed_tokens, cot_panel = gathered(tokens, norm_gain, cotangent)
     count = normed_tokens.shape[0]
     in_factors = jnp.concatenate(
         [

time: 247 us -> 231 us (0.935)
  waiting for transfers between devices: 47.5 us -> 7.36 us
  Pallas kernels: 138 us -> 171 us
  blocking collectives: 11.4 us -> 0 us
  local copies, waits for them, and re-layouts: 14.3 us -> 17.4 us
    all_gather x2 -> x0, waiting for transfers between devices: 34.2 us -> none  [the longest x1 21.8 us: on_device(): cot_panel = lax.all_gather(cotangent, 'col', axis=0, tiled=True)]
    pallas_call x0 -> x1, Pallas kernels: none -> 31.6 us  [gathered(): pl.pallas_call(gather_kernel, out_shape=[jax.ShapeDtypeStruct(whole, jnp....]
    psum x1 -> x0, blocking collectives: 11.4 us -> none  [on_device(): squares = lax.psum(jnp.sum(tokens_f * tokens_f, axis=1), 'row')]
    reduce_scatter x1, waiting for transfers between devices: 12.5 us -> 7.34 us  [on_device(): lax.psum_scatter(feature.astype(jnp.bfloat16).reshape(2, count, width_row...]
    another operation x2, other arithmetic: 0.23 us -> 2.87 us
    unnamed x53 -> x49, local copies, waits for them, and re-layouts: 8.39 us -> 8.38 us
  transfers between devices with their start and end apart: 3 -> 1, of which waited for: 3 -> 1; matrix products, arithmetic and copies ran while one was open for 7% -> 6% of each run, Pallas kernels for 7% -> 9%
where the time goes in v3:
time: 231 us
  Pallas kernels  171 us (74%)
  local copies, waits for them, and re-layouts  17.4 us (8%)
  between operations  14.4 us (6%)
  other arithmetic  10.3 us (4%)
  matrix products  10.2 us (4%)
  waiting for transfers between devices  7.36 us (3%)
    pallas_call x1, Pallas kernels, fused_block(): pl.pallas_call(block_kernel, out_shape=[jax.ShapeDtypeStruct((2 * count,...  106 us
    pallas_call x2, Pallas kernels, shard_total(): pl.pallas_call(functools.partial(total_kernel, axis, n), out_shape=jax.Sh...  33.3 us
    pallas_call x1, Pallas kernels, gathered(): pl.pallas_call(gather_kernel, out_shape=[jax.ShapeDtypeStruct(whole, jnp....  31.6 us
    unnamed x49, local copies, waits for them, and re-layouts  8.38 us
    reduce_scatter x1, waiting for transfers between devices, on_device(): lax.psum_scatter(feature.astype(jnp.bfloat16).reshape(2, count, width_row...  7.34 us
    dot_general x3, matrix products, summed_over_rows(): lax.dot_general(left, right, (((0,), (0,)), ((), ())), preferred_element_...  6.02 us
  transfers between devices with their start and end apart: 1, of which 1 were waited for; matrix products, arithmetic and copies ran while one was open for 6% of the time, Pallas kernels for 9%

profile of v3, /device:TPU:0, one launch (start us, length us, event | category | flops | bytes accessed | tf_op | source)
XLA Modules:
  0.0 230.6 jit_solution(12443555470315412483)
XLA Ops:
  7.2 0.0 reduce-scatter.2.cloned.1.call-start
  7.2 1.0 constant_dynamic-update-slice_fusion.3
  8.2 1.0 constant_dynamic-update-slice_fusion.2
  9.2 0.0 copy-start.15
  9.2 0.0 copy-start.16
  9.2 1.0 constant_dynamic-update-slice_fusion.1
  10.2 1.0 constant_dynamic-update-slice_fusion
  11.2 31.6 %gather.1 = (bf16[8,32,2048]{2,1,0:T(8,128)(2,1)}, bf16[8,32,2048]{2,1,0:T(8,128)(2,1)}) custom-call(bf16[32,2048]{1,0:T(8,128)(2,1)} %tokens.1, f32[1,2048]{1,0:T(1,128)} %bitcast.56, bf16[32,2048]{1,0:T(8,128)(2,1)} %cot.1), custom_call_target="tpu_custom_call" | custom-call | tf_op jit(solution)/shard_map/gather/pallas_call | solution.py:590
  42.8 0.0 copy-start.1
  42.8 1.8 fusion.24
  44.6 0.0 copy-done.15
  44.6 0.0 copy-done.16
  44.6 0.0 copy-done.1
  44.6 0.5 fusion.2
  45.1 0.9 copy.33
  46.1 13.2 %total_row.1 = bf16[4,64,384]{2,1,0:T(8,128)(2,1)} custom-call(f32[4,64,384]{2,1,0:T(8,128)} %bitcast.45), custom_call_target="tpu_custom_call" | custom-call | tf_op jit(solution)/shard_map/total_row/pallas_call | solution.py:91
  59.3 1.0 broadcast_multiply_fusion
  60.2 0.0 copy-start.12
  60.3 0.1 fusion.23
  60.4 0.1 copy.51
  60.5 0.1 copy.52
  60.6 0.6 maximum_bitcast_fusion.2.adj_stack
  61.2 0.1 copy.49
  61.3 0.1 copy.50
  61.4 0.6 maximum_bitcast_fusion.1.up_stack
  62.1 0.1 copy.47
  62.2 0.1 copy.48
  62.3 0.1 copy.46
  62.4 0.0 copy-done.14
  62.4 0.1 broadcast_select_fusion
  62.5 0.6 maximum_bitcast_fusion.gate_stack
  63.1 0.8 copy.43.gate_left
  63.9 0.8 copy.45.adj_left
  64.7 0.8 copy.44.up_left
  65.4 0.4 copy.41
  65.9 0.0 copy-start.8
  65.9 1.5 copy.42
  67.4 0.0 copy-start.9
  67.4 0.0 copy-start.10
  67.4 0.0 copy-start.11
  67.4 1.4 pad_maximum_fusion.2.down_in
  68.8 1.0 pad_maximum_fusion.gate_out
  69.8 1.0 pad_maximum_fusion.1.up_out
  70.8 106.1 %block.1 = (bf16[512,2048]{1,0:T(8,128)(2,1)}, f32[512,128]{1,0:T(8,128)}, f32[512,128]{1,0:T(8,128)}, f32[512,128]{1,0:T(8,128)}, f32[64,3584]{1,0:T(8,128)}, /*index=5*/f32[64,3584]{1,0:T(8,128)}, f32[64,3584]{1,0:T(8,128)}) custom-call(bf16[256,2048]{1,0:T(8,128)(2,1)} %bitcast.36, bf16[256,2048]{1,0:T(8,128)(2,1)} %bitcast.39, ...), custom_call_target="tpu_custom_call" | custom-call | tf_op jit(solution)/shard_map/block/pallas_call | solution.py:403
  176.9 0.0 reduce-scatter.2.cloned.1.call-update
  177.0 1.6 slice.128
  178.6 0.6 slice.127
  179.2 1.2 add_convert_fusion.2
  180.4 1.7 add_convert_fusion
  182.1 1.7 concatenate.98.x_ref
  183.8 20.1 %total_col.1 = bf16[8,32,320]{2,1,0:T(8,128)(2,1)} custom-call(bf16[8,32,320]{2,1,0:T(8,128)(2,1)} %concatenate.98.x_ref), custom_call_target="tpu_custom_call" | custom-call | tf_op jit(solution)/shard_map/total_col/pallas_call | solution.py:91
  203.9 0.7 fusion.22
  204.7 2.0 convolution_multiply_fusion
  206.6 0.0 copy-done
  206.6 2.1 convolution_multiply_fusion.1
  208.7 2.0 convolution_multiply_fusion.2
  210.7 7.3 %reduce-scatter.2.cloned.1.call-done = bf16[2,32,2048]{2,1,0:T(8,128)(2,1)} async-done(((bf16[2,256,2048]{2,1,0:T(8,128)(2,1)}), bf16[2,32,2048]{2,1,0:T(8,128)(2,1)}) %reduce-scatter.2.cloned.1.call-update) | async-done | bytes 262160 | tf_op jit(solution)/shard_map/reduce_scatter | solution.py:749
  218.0 1.0 convert_element_type.5
  219.1 0.9 fusion.1
  220.0 1.0 fusion
  221.0 0.9 copy.59
  221.9 0.9 copy.60
  222.8 0.0 copy-done.5
  222.8 0.9 copy.61
  (25 shorter events, 0.1 us)
Async XLA Ops:
  7.2 210.9 %reduce-scatter.2.cloned.1.call-start = ((), (), s32[]{:S(2)}) async-start(), calls=%async_computation.1 | async-start | bytes 2359296 | tf_op jit(solution)/shard_map/reduce_scatter | solution.py:749
  9.2 35.4 %copy-start.15 = (bf16[64,2048]{1,0:T(8,128)(2,1)S(1)}, bf16[64,2048]{1,0:T(8,128)(2,1)}, u32[]{:S(2)}) copy-start(bf16[64,2048]{1,0:T(8,128)(2,1)} %param.35) | copy-start | bytes 786436
  9.2 35.4 %copy-start.16 = (bf16[64,2048]{1,0:T(8,128)(2,1)S(1)}, bf16[64,2048]{1,0:T(8,128)(2,1)}, u32[]{:S(2)}) copy-start(bf16[64,2048]{1,0:T(8,128)(2,1)} %param.29) | copy-start | bytes 786436
  42.8 1.8 copy-start.1
  46.1 16.3 %copy-start.14 = (pred[128]{0:T(512)(128)(4,1)S(1)}, pred[128]{0:T(512)(128)(4,1)}, u32[]{:S(2)}) copy-start(pred[128]{0:T(512)(128)(4,1)} %constant.8.clone.1) | copy-start | bytes 388
  60.2 5.2 %copy-start.12 = (bf16[3584,64]{0,1:T(8,128)(2,1)S(1)}, bf16[3584,64]{0,1:T(8,128)(2,1)}, u32[]{:S(2)}) copy-start(bf16[3584,64]{0,1:T(8,128)(2,1)} %param.28) | copy-start | bytes 1376260
  65.9 3.0 %copy-start.8 = (bf16[64,3584]{1,0:T(8,128)(2,1)S(1)}, bf16[64,3584]{1,0:T(8,128)(2,1)}, u32[]{:S(2)}) copy-start(bf16[64,3584]{1,0:T(8,128)(2,1)} %param.31) | copy-start | bytes 1376260
  67.4 1.5 copy-start.9
  67.4 2.4 %copy-start.10 = (bf16[64,3584]{1,0:T(8,128)(2,1)S(1)}, bf16[64,3584]{1,0:T(8,128)(2,1)}, u32[]{:S(2)}) copy-start(bf16[64,3584]{1,0:T(8,128)(2,1)} %param.33) | copy-start | bytes 1376260
  67.4 2.4 %copy-start.11 = (bf16[64,3584]{1,0:T(8,128)(2,1)S(1)}, bf16[64,3584]{1,0:T(8,128)(2,1)}, u32[]{:S(2)}) copy-start(bf16[64,3584]{1,0:T(8,128)(2,1)} %param.27) | copy-start | bytes 1376260
  176.9 1.7 copy-start.13
  176.9 27.7 %copy-start.2 = (bf16[8,32,2048]{2,1,0:T(8,128)(2,1)S(1)}, bf16[8,32,2048]{2,1,0:T(8,128)(2,1)}, u32[]{:S(2)}) copy-start(bf16[8,32,2048]{2,1,0:T(8,128)(2,1)} %get-tuple-element.18) | copy-start | bytes 3145732
  179.2 27.4 %copy-start = (bf16[8,32,2048]{2,1,0:T(8,128)(2,1)S(1)}, bf16[8,32,2048]{2,1,0:T(8,128)(2,1)}, u32[]{:S(2)}) copy-start(bf16[8,32,2048]{2,1,0:T(8,128)(2,1)} %get-tuple-element.17) | copy-start | bytes 3145732
  206.6 12.4 %copy-start.3 = (bf16[2048,64]{0,1:T(8,128)(2,1)S(1)}, bf16[2048,64]{0,1:T(8,128)(2,1)}, u32[]{:S(2)}) copy-start(bf16[2048,64]{0,1:T(8,128)(2,1)} %param.24) | copy-start | bytes 786436
  206.6 12.4 %copy-start.4 = (bf16[2048,64]{0,1:T(8,128)(2,1)S(1)}, bf16[2048,64]{0,1:T(8,128)(2,1)}, u32[]{:S(2)}) copy-start(bf16[2048,64]{0,1:T(8,128)(2,1)} %param.26) | copy-start | bytes 786436
  210.7 10.3 %copy-start.7 = (f32[64,3584]{1,0:T(8,128)S(1)}, f32[64,3584]{1,0:T(8,128)}, u32[]{:S(2)}) copy-start(f32[64,3584]{1,0:T(8,128)} %get-tuple-element.47) | copy-start | bytes 2752516
  220.0 1.9 copy-start.6
  221.0 1.9 copy-start.5
Sparse Core Ops, SparseCore 0:
  177.1 40.9 reduce-scatter.1

commit v4 on v3

--- a/solution.py
+++ b/solution.py
@@ -656,7 +656,7 @@
         [curvature_product(normed_tokens, in_factors), cross_shard_total(cot_panel, out_factors)],
         axis=1,
     )
-    ranks = shard_total(projected, "row", 0)
+    ranks = shard_total(projected.astype(jnp.bfloat16), "row", 0)
     gate_out = jnp.concatenate([gate_output_factor, gate_output_factor_direction], axis=0)
     up_out = jnp.concatenate([up_output_factor, up_output_factor_direction], axis=0)
     down_in = jnp.concatenate([down_input_factor, down_input_factor_direction], axis=1)

time: 231 us -> 232 us (level)
  matrix products: 10.2 us -> 13.4 us
    dot_general x3, matrix products: 2.4 us -> 5.25 us  [cross_shard_total(): lax.dot_general(left, right, (((1,), (1,)), ((), ())), preferred_element_...]
    pallas_call x2, Pallas kernels: 33.3 us -> 30.9 us  [shard_total(): pl.pallas_call(functools.partial(total_kernel, axis, n), out_shape=jax.Sh...]
    unnamed x49 -> x56, local copies, waits for them, and re-layouts: 8.38 us -> 9.44 us
where the time goes in v4:
time: 232 us
  Pallas kernels  169 us (73%)
  local copies, waits for them, and re-layouts  16.6 us (7%)
  between operations  14.4 us (6%)
  matrix products  13.4 us (6%)
  other arithmetic  10.9 us (5%)
  waiting for transfers between devices  7.12 us (3%)
    pallas_call x1, Pallas kernels, fused_block(): pl.pallas_call(block_kernel, out_shape=[jax.ShapeDtypeStruct((2 * count,...  106 us
    pallas_call x1, Pallas kernels, gathered(): pl.pallas_call(gather_kernel, out_shape=[jax.ShapeDtypeStruct(whole, jnp....  31.8 us
    pallas_call x2, Pallas kernels, shard_total(): pl.pallas_call(functools.partial(total_kernel, axis, n), out_shape=jax.Sh...  30.9 us
    unnamed x56, local copies, waits for them, and re-layouts  9.44 us
    reduce_scatter x1, waiting for transfers between devices, on_device(): lax.psum_scatter(feature.astype(jnp.bfloat16).reshape(2, count, width_row...  7.1 us
    dot_general x3, matrix products, summed_over_rows(): lax.dot_general(left, right, (((0,), (0,)), ((), ())), preferred_element_...  6.08 us
    dot_general x3, matrix products, cross_shard_total(): lax.dot_general(left, right, (((1,), (1,)), ((), ())), preferred_element_...  5.25 us
  transfers between devices with their start and end apart: 1, of which 1 were waited for; matrix products, arithmetic and copies ran while one was open for 6% of the time, Pallas kernels for 9%

profile of v4, /device:TPU:0, one launch (start us, length us, event | category | flops | bytes accessed | tf_op | source)
XLA Modules:
  0.0 231.6 jit_solution(13960803446107135077)
XLA Ops:
  7.2 0.0 reduce-scatter.2.cloned.1.call-start
  7.2 1.3 copy.36
  8.5 1.2 copy.37
  9.8 1.2 copy.38
  11.0 0.0 copy-done.16
  11.0 0.0 copy-start.7
  11.0 0.3 copy.39
  11.3 31.8 %gather.1 = (bf16[8,32,2048]{2,1,0:T(8,128)(2,1)}, bf16[8,32,2048]{2,1,0:T(8,128)(2,1)}) custom-call(bf16[32,2048]{1,0:T(8,128)(2,1)} %tokens.1, f32[1,2048]{1,0:T(1,128)} %bitcast.60, bf16[32,2048]{1,0:T(8,128)(2,1)} %cot.1), custom_call_target="tpu_custom_call" | custom-call | tf_op jit(solution)/shard_map/gather/pallas_call | solution.py:590
  43.1 0.0 copy-done.19
  43.1 0.0 copy-done.18
  43.1 1.7 convolution_convert_fusion.1
  44.8 2.1 convolution_convert_fusion
  46.9 0.0 copy-start.17
  46.9 0.7 pad_maximum_fusion.4.x_ref
  47.6 11.0 %total_row.1 = bf16[4,64,384]{2,1,0:T(8,128)(2,1)} custom-call(bf16[4,64,384]{2,1,0:T(8,128)(2,1)} %pad_maximum_fusion.4.x_ref), custom_call_target="tpu_custom_call" | custom-call | tf_op jit(solution)/shard_map/total_row/pallas_call | solution.py:91
  58.6 0.0 copy-start.14
  58.7 1.0 broadcast_multiply_fusion
  59.7 0.1 fusion.22
  59.8 0.1 copy.57
  59.9 0.1 copy.58
  60.0 0.6 maximum_bitcast_fusion.4.adj_stack
  60.7 0.1 copy.55
  60.8 0.1 copy.56
  60.8 0.6 maximum_bitcast_fusion.3.up_stack
  61.5 0.1 copy.53
  61.6 0.1 copy.54
  61.7 0.1 copy.52
  61.8 0.0 copy-done.17
  61.8 0.1 broadcast_select_fusion
  61.9 0.6 maximum_bitcast_fusion.2.gate_stack
  62.6 0.8 copy.49.gate_left
  63.3 0.8 copy.51.adj_left
  64.1 0.8 copy.50.up_left
  64.8 0.4 copy.47
  65.3 0.0 copy-start.10
  65.3 1.5 copy.48
  66.8 0.0 copy-start.11
  66.8 0.0 copy-start.12
  66.8 0.0 copy-start.13
  66.8 1.4 pad_maximum_fusion.3.down_in
  68.3 1.0 pad_maximum_fusion.1.gate_out
  69.2 1.0 pad_maximum_fusion.2.up_out
  70.2 106.4 %block.1 = (bf16[512,2048]{1,0:T(8,128)(2,1)}, f32[512,128]{1,0:T(8,128)}, f32[512,128]{1,0:T(8,128)}, f32[512,128]{1,0:T(8,128)}, f32[64,3584]{1,0:T(8,128)}, /*index=5*/f32[64,3584]{1,0:T(8,128)}, f32[64,3584]{1,0:T(8,128)}) custom-call(bf16[256,2048]{1,0:T(8,128)(2,1)} %bitcast.41, bf16[256,2048]{1,0:T(8,128)(2,1)} %bitcast.45, ...), custom_call_target="tpu_custom_call" | custom-call | tf_op jit(solution)/shard_map/block/pallas_call | solution.py:403
  176.6 0.0 copy-start.15
  176.6 0.0 copy-start.1
  176.7 0.0 reduce-scatter.2.cloned.1.call-update
  176.7 1.7 slice.128
  178.4 0.6 slice.127
  179.0 1.1 add_convert_fusion.2
  180.1 1.7 add_convert_fusion
  181.8 1.7 concatenate.100.x_ref
  183.5 19.9 %total_col.1 = bf16[8,32,320]{2,1,0:T(8,128)(2,1)} custom-call(bf16[8,32,320]{2,1,0:T(8,128)(2,1)} %concatenate.100.x_ref), custom_call_target="tpu_custom_call" | custom-call | tf_op jit(solution)/shard_map/total_col/pallas_call | solution.py:91
  203.5 0.7 fusion.21
  204.2 2.0 convolution_multiply_fusion
  206.1 2.1 convolution_multiply_fusion.1
  208.2 2.0 convolution_multiply_fusion.2
  210.3 7.1 %reduce-scatter.2.cloned.1.call-done = bf16[2,32,2048]{2,1,0:T(8,128)(2,1)} async-done(((bf16[2,256,2048]{2,1,0:T(8,128)(2,1)}), bf16[2,32,2048]{2,1,0:T(8,128)(2,1)}) %reduce-scatter.2.cloned.1.call-update) | async-done | bytes 262160 | tf_op jit(solution)/shard_map/reduce_scatter | solution.py:749
  217.4 1.0 convert_element_type.7
  218.4 0.0 copy-done.2
  218.4 0.9 fusion.1
  219.3 2.7 %fusion = f32[32,2048]{1,0:T(8,128)} fusion(f32[2,32,2048]{2,1,0:T(8,128)S(1)} %convert_element_type.7, bf16[32,128]{1,0:T(8,128)(2,1)S(1)} %get-tuple-element.27, bf16[32,128]{1,0:T(8,128)(2,1)S(1)} %get-tuple-element.26, bf16[2048,64]{1,0:T(8,128)(2,1)} %copy-done.9, bf16[2048,64]{1,0:T(8,128)(2,1)S(1)} %copy-done.8, bf16[2048,64]{1,0:T(8,128)(2,1)S(1)} %copy.37, ...), kind=kOutput, calls=%fused_computation.4 | convolution fusion | flops 37912576 | bytes 1589248 | tf_op jit(solution)/shard_map/dot_general | solution.py:115
  222.0 0.9 copy.62
  222.9 0.9 copy.63
  223.8 0.9 copy.64
  (30 shorter events, 0.1 us)
Async XLA Ops:
  7.2 3.8 %copy-start.16 = (bf16[2048,64]{0,1:T(8,128)(2,1)S(1)}, bf16[2048,64]{0,1:T(8,128)(2,1)}, u32[]{:S(2)}) copy-start(bf16[2048,64]{0,1:T(8,128)(2,1)} %param.32) | copy-start | bytes 786436
  7.2 35.9 %copy-start.19 = (bf16[64,2048]{1,0:T(8,128)(2,1)S(1)}, bf16[64,2048]{1,0:T(8,128)(2,1)}, u32[]{:S(2)}) copy-start(bf16[64,2048]{1,0:T(8,128)(2,1)} %param.29) | copy-start | bytes 786436
  7.2 35.9 %copy-start.18 = (bf16[64,2048]{1,0:T(8,128)(2,1)S(1)}, bf16[64,2048]{1,0:T(8,128)(2,1)}, u32[]{:S(2)}) copy-start(bf16[64,2048]{1,0:T(8,128)(2,1)} %param.35) | copy-start | bytes 786436
  7.2 210.2 %reduce-scatter.2.cloned.1.call-start = ((), (), s32[]{:S(2)}) async-start(), calls=%async_computation.1 | async-start | bytes 2359296 | tf_op jit(solution)/shard_map/reduce_scatter | solution.py:749
  11.0 35.9 %copy-start.7 = (bf16[2048,64]{1,0:T(8,128)(2,1)}, bf16[2048,64]{1,0:T(8,128)(2,1)S(1)}, u32[]{:S(2)}) copy-start(bf16[2048,64]{1,0:T(8,128)(2,1)S(1)} %copy.38) | copy-start | bytes 786436
  11.3 35.6 %copy-start.9 = (bf16[2048,64]{1,0:T(8,128)(2,1)}, bf16[2048,64]{1,0:T(8,128)(2,1)S(1)}, u32[]{:S(2)}) copy-start(bf16[2048,64]{1,0:T(8,128)(2,1)S(1)} %copy.39) | copy-start | bytes 786436
  46.9 14.9 %copy-start.17 = (pred[128]{0:T(512)(128)(4,1)S(1)}, pred[128]{0:T(512)(128)(4,1)}, u32[]{:S(2)}) copy-start(pred[128]{0:T(512)(128)(4,1)} %constant.8.clone.1) | copy-start | bytes 388
  58.6 6.2 %copy-start.14 = (bf16[3584,64]{0,1:T(8,128)(2,1)S(1)}, bf16[3584,64]{0,1:T(8,128)(2,1)}, u32[]{:S(2)}) copy-start(bf16[3584,64]{0,1:T(8,128)(2,1)} %param.28) | copy-start | bytes 1376260
  65.3 3.0 %copy-start.10 = (bf16[64,3584]{1,0:T(8,128)(2,1)S(1)}, bf16[64,3584]{1,0:T(8,128)(2,1)}, u32[]{:S(2)}) copy-start(bf16[64,3584]{1,0:T(8,128)(2,1)} %param.31) | copy-start | bytes 1376260
  66.8 1.5 copy-start.11
  66.8 2.4 %copy-start.12 = (bf16[64,3584]{1,0:T(8,128)(2,1)S(1)}, bf16[64,3584]{1,0:T(8,128)(2,1)}, u32[]{:S(2)}) copy-start(bf16[64,3584]{1,0:T(8,128)(2,1)} %param.33) | copy-start | bytes 1376260
  66.8 2.4 %copy-start.13 = (bf16[64,3584]{1,0:T(8,128)(2,1)S(1)}, bf16[64,3584]{1,0:T(8,128)(2,1)}, u32[]{:S(2)}) copy-start(bf16[64,3584]{1,0:T(8,128)(2,1)} %param.27) | copy-start | bytes 1376260
  176.6 1.8 copy-start.15
  176.6 27.5 %copy-start.1 = (bf16[8,32,2048]{2,1,0:T(8,128)(2,1)S(1)}, bf16[8,32,2048]{2,1,0:T(8,128)(2,1)}, u32[]{:S(2)}) copy-start(bf16[8,32,2048]{2,1,0:T(8,128)(2,1)} %get-tuple-element.18) | copy-start | bytes 3145732
  176.7 29.5 %copy-start = (bf16[8,32,2048]{2,1,0:T(8,128)(2,1)S(1)}, bf16[8,32,2048]{2,1,0:T(8,128)(2,1)}, u32[]{:S(2)}) copy-start(bf16[8,32,2048]{2,1,0:T(8,128)(2,1)} %get-tuple-element.17) | copy-start | bytes 3145732
  206.1 12.2 %copy-start.2 = (bf16[2048,64]{0,1:T(8,128)(2,1)S(1)}, bf16[2048,64]{0,1:T(8,128)(2,1)}, u32[]{:S(2)}) copy-start(bf16[2048,64]{0,1:T(8,128)(2,1)} %param.26) | copy-start | bytes 786436
  206.1 12.2 %copy-start.3 = (bf16[2048,64]{0,1:T(8,128)(2,1)S(1)}, bf16[2048,64]{0,1:T(8,128)(2,1)}, u32[]{:S(2)}) copy-start(bf16[2048,64]{0,1:T(8,128)(2,1)} %param.24) | copy-start | bytes 786436
  208.2 11.1 %copy-start.8 = (bf16[2048,64]{1,0:T(8,128)(2,1)S(1)}, bf16[2048,64]{1,0:T(8,128)(2,1)}, u32[]{:S(2)}) copy-start(bf16[2048,64]{1,0:T(8,128)(2,1)} %copy-done.7) | copy-start | bytes 786436
  219.3 2.7 %copy-start.6 = (f32[64,3584]{1,0:T(8,128)S(1)}, f32[64,3584]{1,0:T(8,128)}, u32[]{:S(2)}) copy-start(f32[64,3584]{1,0:T(8,128)} %get-tuple-element.47) | copy-start | bytes 2752516
  219.3 3.6 %copy-start.5 = (f32[64,3584]{1,0:T(8,128)S(1)}, f32[64,3584]{1,0:T(8,128)}, u32[]{:S(2)}) copy-start(f32[64,3584]{1,0:T(8,128)} %get-tuple-element.49) | copy-start | bytes 2752516
  222.0 1.9 copy-start.4
Sparse Core Ops, SparseCore 0:
  176.8 40.5 reduce-scatter.1
